TPU v7x, 32 devices: a whole 2x2x4 slice. The times are simulated.
32 devices in a mesh: half: 2 (over x), grid: 2 (over y), dom: 8 (over z, core).
Axes of the slice: x: 2, y: 2, z: 4, core: 2. Of those that a mesh axis runs over, the one named last changes fastest.
Arguments:
- grids: float32 [16, 64, 64, 4096], P(('half', 'grid'), 'dom'), may hold values from -0.8 to 0.8
- levels: int32 [16, 4], replicated, may hold values from 4 to 6, as said below
Outputs:
- combined: float32 [16, 64, 64, 4096], P(('half', 'grid'), 'dom')
Inputs may be any that keep to these rules, and one draw needn't show every extreme that they name: `levels`: with base b = (4, 5, 5, 5), rows 0 to 7 are b plus, in some order, (2,1,1,0), (2,1,0,1), (2,0,1,1), (1,1,1,1), (1,1,0,0), (1,0,1,0), (1,0,0,1), (0,0,0,0); rows 8 to 15 are b plus, in some order, (2,1,0,0), (2,0,1,0), (2,0,0,1), (1,1,1,0), (1,1,0,1), (1,0,1,1), (2,0,0,0), (1,0,0,0).
All inputs are finite; a program needn't handle non-finite values.
Results may differ from a plain program's by a relative error of at most 0.0003.
Values sent between devices are 32-bit elements; how exact they have to be, the bound alone decides.
No kernel may reach another device: no remote copies, remote signals or barrier semaphores. Data moves between devices by JAX's collectives and lax.ppermute only.
A program may use at most 320 MiB of HBM per device.

v0:
```python
import jax
import jax.numpy as jnp
import numpy as np
from jax import lax
from jax.experimental import pallas as pl
from jax.experimental.pallas import tpu as pltpu
from jax.sharding import PartitionSpec as P


LEV1 = 6
LEV2 = 6
LEV3 = 6
LEV4 = 6
N1 = 64
N2 = 64
N3 = 64
N4 = 64
SPANS = (2, 1, 1, 1)


BLOCKS = (
    (0, 0, 0), (1, 0, 0), (0, 1, 0), (0, 0, 1),
    (1, 1, 0), (1, 0, 1), (0, 1, 1), (1, 1, 1),
)
SHARED_D = 4
SHARED_C = 7
HB = N2 // 2
HC = N3 // 2
HD = N4 // 2
GROUPS = 8
CG = N3 // GROUPS
LANES = HC * HD
HALF_LANES = LANES // 2
QR = HB // 4
TILE = CG // 2 * HD
SLOTS = tuple((h, sx, sy) for h in range(2) for sx in range(2) for sy in range(2))


def combination_weights(levels):
    corners = np.array(
        [[corner >> place & 1 for place in range(4)] for corner in range(16)], dtype=np.int32
    )
    parity = 1 - 2 * (corners.sum(axis=1) % 2)
    raised = levels[:, None, :] + jnp.asarray(corners, dtype=jnp.int32)[None, :, :]
    below = jnp.all(raised[:, :, None, :] <= levels[None, None, :, :], axis=3)
    inside = jnp.any(below, axis=2).astype(jnp.int32)
    return jnp.sum(inside * jnp.asarray(parity, dtype=jnp.int32)[None, :], axis=1)


def split_matrix(count_in, half, wrap):
    table = np.zeros((count_in, 2, half))
    for k in range(half):
        table[2 * k, 0, k] = 1.0
        table[2 * k + 1, 1, k] += 1.0
        table[2 * k, 1, k] -= 0.5
        table[(2 * k + 2) % wrap, 1, k] -= 0.5
    return table


def plain_matrix(count_in, half):
    table = np.zeros((count_in, 1, half))
    for k in range(half):
        table[k, 0, k] = 1.0
    return table


def join_matrix(parts_in, half_out, wrap, next_points):
    table = np.zeros((parts_in, half_out + next_points, 2 * half_out))
    for k in range(half_out):
        table[0, k, 2 * k] = 1.0
        table[1, k, 2 * k + 1] += 1.0
        table[0, k, 2 * k + 1] += 0.5
        table[0, (k + 1) % wrap, 2 * k + 1] += 0.5
    return table


def forward_tables():
    half_c = CG // 2
    tables = {}
    for oc in range(2):
        for od in range(2):
            if oc:
                along_c = split_matrix(CG + 2, half_c, CG + 2)
            else:
                along_c = plain_matrix(half_c, half_c)
            along_d = split_matrix(N4, HD, N4) if od else plain_matrix(N4, HD)
            table = np.einsum("cpk,dql->cdpqkl", along_c, along_d)
            rows = along_c.shape[0] * N4
            tables[oc, od] = jnp.asarray(table.reshape(rows, -1), jnp.bfloat16)
    return tables


def backward_tables():
    half_c = CG // 2
    tables = {}
    for oc in range(2):
        for od in range(2):
            if od:
                along_d = join_matrix(2, HD, HD, 0)
            else:
                along_d = np.zeros((1, HD, N4))
                along_d[0, np.arange(HD), np.arange(HD)] = 1.0
            if oc:
                along_c = join_matrix(2, half_c, half_c + half_c, half_c)
                own = np.einsum("pkc,qld->pqklcd", along_c[:, :half_c], along_d)
                ahead = np.einsum("pkc,qld->pqklcd", along_c[:1, half_c:], along_d)
                cols = CG * N4
                table = np.concatenate([own.reshape(-1, cols), ahead.reshape(-1, cols)], axis=0)
            else:
                along_c = np.eye(half_c)[None]
                table = np.einsum("pkc,qld->pqklcd", along_c, along_d).reshape(-1, half_c * N4)
            tables[oc, od] = jnp.asarray(table, jnp.bfloat16)
    return tables


CASES = ((0, 0), (0, 1), (1, 0), (1, 1))


def split_parts(value):
    high = value.astype(jnp.bfloat16)
    low = (value - high.astype(jnp.float32)).astype(jnp.bfloat16)
    return high, low


def grid_facts(scal, g):
    return tuple(scal[4 * g + axis] for axis in range(4))


def forward_kernel(fine, rows_here, count, scal, fetch, weight, x_ref, *refs):
    tables = dict(zip(CASES, refs[:4]))
    outs = refs[4:-2]
    xb, yb = refs[-2:]
    half_rows = rows_here // 2
    i = pl.program_id(0)
    g = pl.program_id(1)
    level, fine_b, fine_c, fine_d = grid_facts(scal, g)
    mine_x = scal[4 * count]
    mine_y = scal[4 * count + 1]
    row = scal[4 * count + 2] + i
    odd = lax.rem(i, 2) == 1
    even = lax.rem(i, 2) == 0
    active = row < (N1 // 4) * (1 << level)
    active = active & (level == (2 if fine else 1))

    def clear(wanted, *targets):
        @pl.when((g == 0) & wanted)
        def _():
            for target in targets:
                target[...] = jnp.zeros_like(target)

    if fine:
        e6 = dict(zip(SLOTS, outs[:8]))
        d6 = dict(zip(SLOTS, outs[8:16]))
        e6_rest, d6_self = outs[16:]
        clear(even, *outs[:8], e6_rest)
        clear(odd, *outs[8:16], d6_self)
    else:
        s5 = dict(zip(SLOTS, outs[:8]))
        s5_low, s5_high, s5_self = outs[8:]
        clear(i >= 0, *outs[:8], s5_self)
        clear(i < half_rows, s5_low)
        clear(i >= half_rows, s5_high)

    def put(values, fine_c_here):
        rows = slice(0, values.shape[0])
        high, low = split_parts(values)
        span = CG * N4 if fine_c_here else CG // 2 * N4
        reach = span + 2 * N4 if fine_c_here else span
        for k in range(GROUPS):
            for place, piece in ((0, high), (reach, low)):
                xb[k, rows, place : place + span] = piece[:, k * span : k * span + span]
                if fine_c_here:
                    ahead = (k + 1) % GROUPS * span
                    xb[k, rows, place + span : place + reach] = piece[:, ahead : ahead + 2 * N4]

    for oc, od in CASES:
        for ob in range(2):
            @pl.when(active & (fine_b == ob) & (fine_c == oc) & (fine_d == od))
            def _(oc=oc, od=od, ob=ob):
                lanes = N3 * N4 if oc else HC * N4
                rows = (1 + ob) * HB
                put(x_ref[0, 0, :rows, :lanes], oc)
                reach = (CG + 2) * N4 if oc else CG // 2 * N4
                table = tables[oc, od][...]
                lhs = xb[:, :rows, : 2 * reach].reshape(GROUPS * rows, 2 * reach)
                result = jnp.dot(
                    lhs[:, :reach], table, preferred_element_type=jnp.float32
                ) + jnp.dot(lhs[:, reach:], table, preferred_element_type=jnp.float32)
                for pc in range(oc + 1):
                    for pd in range(od + 1):
                        column = (pc * (od + 1) + pd) * TILE
                        for k in range(GROUPS):
                            piece = result[k * rows : k * rows + rows, column : column + TILE]
                            if ob:
                                yb[2 * pc + pd, k, :N2] = piece
                                yb[2 * pc + pd, k, N2:] = piece[:QR]
                            else:
                                yb[2 * pc + pd, k, pl.ds(0, HB, stride=2)] = piece

    scale = weight[g]

    def add_up(wanted, blocks, target):
        for block in blocks:
            pb, pc, pd = BLOCKS[block]

            @pl.when(wanted & (pb <= fine_b) & (pc <= fine_c) & (pd <= fine_d))
            def _(block=block, pb=pb, part=2 * pc + pd):
                for h, sx, sy in SLOTS:
                    quarter = 2 * (sx ^ mine_x) + (sy ^ mine_y)
                    start = pl.multiple_of(quarter * 2 * QR, 2 * QR)
                    ref, index = target(block, h, sx, sy)
                    for j in range(GROUPS // 2):
                        k = h * (GROUPS // 2) + j
                        piece = yb[part, k, pl.ds(start, QR, stride=2)]
                        if pb:
                            piece = yb[part, k, pl.ds(start + 1, QR, stride=2)] - 0.5 * (
                                piece + yb[part, k, pl.ds(start + 2, QR, stride=2)]
                            )
                        where = index + (slice(None), slice(j * TILE, j * TILE + TILE))
                        ref[where] += scale * piece

    def slot_of(parts):
        return lambda block, h, sx, sy: (parts[h, sx, sy], (block, 0))

    def rest_of(ref):
        return lambda block, h, sx, sy: (ref, (h, sx, sy, block - SHARED_D, 0))

    def line_of(ref):
        return lambda block, h, sx, sy: (ref, (h, sx, sy, 0))

    if fine:
        add_up(active & even, range(SHARED_D), slot_of(e6))
        add_up(active & even, range(SHARED_D, SHARED_C), rest_of(e6_rest))
        add_up(active & odd, range(SHARED_D), slot_of(d6))
        add_up(active & odd, range(SHARED_D, SHARED_C), rest_of(d6_self))

        @pl.when((g == count - 1) & (i > 0))
        def _():
            for slot in SLOTS:
                d6[slot][...] -= 0.5 * e6[slot][...]
            d6_self[...] -= 0.5 * e6_rest[...]
    else:
        five = active
        add_up(five, range(SHARED_D), slot_of(s5))
        add_up(five & (i < half_rows), range(SHARED_D, SHARED_C), rest_of(s5_low))
        add_up(five & (i >= half_rows), range(SHARED_D, SHARED_C), rest_of(s5_high))
        add_up(five, range(SHARED_C, 8), line_of(s5_self))


def forward(fine, grids, scal, weight):
    count, rows_here = grids.shape[:2]
    half_rows = rows_here // 2
    tables = forward_tables()
    levels = scal[: 4 * count].reshape(count, 4)[:, 0]
    rows = scal[4 * count + 2] + jnp.arange(rows_here, dtype=jnp.int32)
    takes = levels == (2 if fine else 1)
    takes = takes[None, :] & (rows[:, None] < (N1 // 4) * (1 << levels)[None, :])
    steps = jnp.arange(rows_here * count, dtype=jnp.int32)
    earlier = (steps[None, :] <= steps[:, None]) & takes.reshape(-1)[None, :]
    fetch = jnp.max(jnp.where(earlier, steps[None, :], 0), axis=1)

    def constant(table):
        return pl.BlockSpec(table.shape, lambda i, g, *_: (0, 0))

    def page(i, g, scal, fetch, weight):
        step = fetch[i * count + g]
        return (lax.rem(step, count), step // count, 0, 0)

    def rows_spec(blocks, row_of):
        return pl.BlockSpec(
            (blocks, 1, QR, HALF_LANES), lambda i, g, *_: (0, row_of(i), 0, 0)
        )

    def shape(*dims):
        return jax.ShapeDtypeStruct(dims + (QR, HALF_LANES), jnp.float32)

    def even_row(i):
        return i // 2

    def odd_row(i):
        return jnp.maximum(i - 1, 0) // 2

    rest = SHARED_C - SHARED_D
    if fine:
        out_specs = (
            [rows_spec(SHARED_D, even_row)] * 8
            + [rows_spec(SHARED_D, odd_row)] * 8
            + [rest_spec(rest, even_row), rest_spec(rest, odd_row)]
        )
        out_shape = [shape(SHARED_D, half_rows)] * 16 + [shape(2, 2, 2, rest, half_rows)] * 2
    else:
        out_specs = [rows_spec(SHARED_D, lambda i: i)] * 8 + [
            rest_spec(rest, lambda i: jnp.minimum(i, half_rows - 1)),
            rest_spec(rest, lambda i: jnp.maximum(i - half_rows, 0)),
            line_spec(lambda i: i),
        ]
        out_shape = (
            [shape(SHARED_D, rows_here)] * 8
            + [shape(2, 2, 2, rest, half_rows)] * 2
            + [shape(2, 2, 2, rows_here)]
        )
    ordered = [tables[case] for case in CASES]
    return pl.pallas_call(
        lambda *refs: forward_kernel(fine, rows_here, count, *refs),
        grid_spec=pltpu.PrefetchScalarGridSpec(
            num_scalar_prefetch=3,
            grid=(rows_here, count),
            in_specs=[pl.BlockSpec((1, 1, N2, N3 * N4), page)]
            + [constant(table) for table in ordered],
            out_specs=out_specs,
            scratch_shapes=[
                pltpu.VMEM((GROUPS, 2 * HB, 2 * (CG + 2) * N4), jnp.bfloat16),
                pltpu.VMEM((4, GROUPS, N2 + QR, TILE), jnp.float32),
            ],
        ),
        out_shape=out_shape,
        compiler_params=pltpu.CompilerParams(vmem_limit_bytes=60 * 2**20),
        cost_estimate=pl.CostEstimate(
            flops=10**10, bytes_accessed=60 * 2**20, transcendentals=0
        ),
        name="split_fine" if fine else "split_coarse",
    )(scal, fetch, weight, grids, *ordered)


def coarsest_kernel(count, scal, weight, x_ref, table, out, yb):
    i = pl.program_id(0)
    g = pl.program_id(1)
    mine_x = scal[4 * count]
    mine_y = scal[4 * count + 1]
    active = (scal[4 * g] == 0) & (scal[4 * count + 2] + i < N1 // 4)

    @pl.when(g == 0)
    def _():
        out[...] = jnp.zeros_like(out)

    @pl.when(active)
    def _():
        span = CG // 2 * N4
        for k in range(GROUPS):
            high, low = split_parts(x_ref[0, 0, :, k * span : k * span + span])
            yb[k] = weight[g] * (
                jnp.dot(high, table[...], preferred_element_type=jnp.float32)
                + jnp.dot(low, table[...], preferred_element_type=jnp.float32)
            )
        for h, sx, sy in SLOTS:
            quarter = 2 * (sx ^ mine_x) + (sy ^ mine_y)
            start = pl.multiple_of(quarter * QR, QR)
            for j in range(GROUPS // 2):
                out[h, sx, sy, 0, :, j * TILE : j * TILE + TILE] += yb[
                    h * (GROUPS // 2) + j, pl.ds(start, QR)
                ]


def coarsest(grids, scal, weight):
    count, rows_here = grids.shape[:2]
    table = forward_tables()[0, 0]

    def page(i, g, scal, weight):
        wanted = (scal[4 * g] == 0) & (scal[4 * count + 2] + i < N1 // 4)
        return (jnp.where(wanted, g, 0), jnp.where(wanted, i, 0), 0, 0)

    return pl.pallas_call(
        lambda *refs: coarsest_kernel(count, *refs),
        grid_spec=pltpu.PrefetchScalarGridSpec(
            num_scalar_prefetch=2,
            grid=(rows_here, count),
            in_specs=[
                pl.BlockSpec((1, 1, HB, HC * N4), page),
                pl.BlockSpec(table.shape, lambda i, g, *_: (0, 0)),
            ],
            out_specs=line_spec(lambda i: i),
            scratch_shapes=[pltpu.VMEM((GROUPS, HB, TILE), jnp.float32)],
        ),
        out_shape=jax.ShapeDtypeStruct((2, 2, 2, rows_here, QR, HALF_LANES), jnp.float32),
        compiler_params=pltpu.CompilerParams(vmem_limit_bytes=60 * 2**20),
        cost_estimate=pl.CostEstimate(
            flops=10**8, bytes_accessed=4 * 2**20, transcendentals=0
        ),
        name="split_coarsest",
    )(scal, weight, grids, table)


def rest_spec(blocks, row_of):
    return pl.BlockSpec(
        (2, 2, 2, blocks, 1, QR, HALF_LANES), lambda i, g, *_: (0, 0, 0, 0, row_of(i), 0, 0)
    )


def line_spec(row_of):
    return pl.BlockSpec(
        (2, 2, 2, 1, QR, HALF_LANES), lambda i, g, *_: (0, 0, 0, row_of(i), 0, 0)
    )


def backward_kernel(fine, rows_here, count, scal, order, *refs):
    used = 7 if fine else 20
    c6, c6_next, c6_rest, c6_rest_next, ahead_row, d6, d6_self = refs[:7]
    if not fine:
        c5 = dict(zip(SLOTS, refs[7:15]))
        c5_low, c5_high, s5_self = refs[15:18]
        c4 = refs[18]
    tables = dict(zip(CASES, refs[used : used + 4]))
    out = refs[used + 4]
    coarse, detail, joined, xb = refs[used + 5 :]
    half_rows = rows_here // 2
    i = pl.program_id(0)
    slot_number = pl.program_id(1)
    g = order[slot_number]
    level, fine_b, fine_c, fine_d = grid_facts(scal, g)
    mine_x = scal[4 * count]
    mine_y = scal[4 * count + 1]
    row = scal[4 * count + 2] + i
    odd = lax.rem(i, 2) == 1
    even = lax.rem(i, 2) == 0
    fresh = slot_number < order[count]
    inside = row < (N1 // 4) * (1 << level)
    active = fresh & inside

    def stage(wanted, blocks, source):
        for block in blocks:
            pb, pc, pd = BLOCKS[block]

            @pl.when(active & wanted & (pb <= fine_b) & (pc <= fine_c) & (pd <= fine_d))
            def _(block=block, work=(coarse, detail)[pb], part=2 * pc + pd):
                for h, sx, sy in SLOTS:
                    quarter = 2 * (sx ^ mine_x) + (sy ^ mine_y)
                    start = pl.multiple_of(quarter * QR, QR)
                    value = source(block, h, sx, sy)
                    for j in range(GROUPS // 2):
                        k = h * (GROUPS // 2) + j
                        work[part, k, pl.ds(start, QR)] = value[:, j * TILE : j * TILE + TILE]

    def here(block, h, sx, sy):
        if block < SHARED_D:
            return c6[h, sx, sy, block, 0]
        return c6_rest[h, sx, sy, block - SHARED_D, 0]

    def between(last):
        def value(block, h, sx, sy):
            if last:
                after = ahead_row[h, sx, sy, block, 0]
            elif block < SHARED_D:
                after = c6_next[h, sx, sy, block, 0]
            else:
                after = c6_rest_next[h, sx, sy, block - SHARED_D, 0]
            mean = 0.5 * (here(block, h, sx, sy) + after)
            if block < SHARED_D:
                return mean + d6[h, sx, sy, block, 0]
            return mean + d6_self[h, sx, sy, block - SHARED_D, 0]

        return value

    stage((level == 2) & even, range(SHARED_C), here)
    if half_rows > 1:
        stage((level == 2) & odd & (i < rows_here - 1), range(SHARED_C), between(False))
    stage((level == 2) & odd & (i == rows_here - 1), range(SHARED_C), between(True))
    if not fine:
        rest = range(SHARED_D, SHARED_C)
        five = level == 1
        stage(five, range(SHARED_D), lambda b, h, x, y: c5[h, x, y][b, 0])
        stage(five & (i < half_rows), rest, lambda b, h, x, y: c5_low[h, x, y, b - SHARED_D, 0])
        stage(five & (i >= half_rows), rest, lambda b, h, x, y: c5_high[h, x, y, b - SHARED_D, 0])
        stage(five, range(SHARED_C, 8), lambda b, h, x, y: s5_self[h, x, y, 0])
        stage(level == 0, range(1), lambda b, h, x, y: c4[h, x, y, 0])

    @pl.when(fresh & jnp.logical_not(inside))
    def _():
        out[...] = jnp.zeros_like(out)

    for oc, od in CASES:
        for ob in range(2):
            @pl.when(active & (fine_b == ob) & (fine_c == oc) & (fine_d == od))
            def _(oc=oc, od=od, ob=ob):
                parts = [(pc, pd) for pc in range(oc + 1) for pd in range(od + 1)]
                ahead = [(0, pd) for pd in range(od + 1)] if oc else []
                reach = (len(parts) + len(ahead)) * TILE
                rows = (1 + ob) * HB
                for place, (pc, pd) in enumerate(parts):
                    part = 2 * pc + pd
                    for k in range(GROUPS):
                        value = coarse[part, k, :HB]
                        if ob:
                            coarse[part, k, HB:] = coarse[part, k, :QR]
                            mean = 0.5 * (value + coarse[part, k, 1 : HB + 1])
                            joined[k, pl.ds(0, HB, stride=2)] = value
                            joined[k, pl.ds(1, HB, stride=2)] = detail[part, k] + mean
                            value = joined[k]
                        for base, piece in zip((0, reach), split_parts(value)):
                            start = base + place * TILE
                            xb[k, :rows, start : start + TILE] = piece
                            if oc and not pc:
                                start = base + (len(parts) + pd) * TILE
                                before = (k + GROUPS - 1) % GROUPS
                                xb[before, :rows, start : start + TILE] = piece
                table = tables[oc, od][...]
                lhs = xb[:, :rows, : 2 * reach].reshape(GROUPS * rows, 2 * reach)
                result = jnp.dot(
                    lhs[:, :reach], table, preferred_element_type=jnp.float32
                ) + jnp.dot(lhs[:, reach:], table, preferred_element_type=jnp.float32)
                span = CG * N4 if oc else CG // 2 * N4
                for k in range(GROUPS):
                    out[0, 0, :rows, k * span : k * span + span] = result[
                        k * rows : k * rows + rows
                    ]
                if not ob:
                    out[0, 0, HB:, :] = jnp.zeros((HB, N3 * N4), jnp.float32)
                if not oc:
                    out[0, 0, :, HC * N4 :] = jnp.zeros((N2, HC * N4), jnp.float32)


def backward(fine, count, scal, rows_here, values, before=None):
    half_rows = rows_here // 2
    tables = backward_tables()
    ordered = [tables[case] for case in CASES]
    levels = scal[: 4 * count].reshape(count, 4)[:, 0]
    takes = (levels == 2) if fine else (levels < 2)
    number = jnp.maximum(jnp.sum(takes.astype(jnp.int32)), 1)
    spots = jnp.arange(count, dtype=jnp.int32)
    before_me = (spots[None, :] < spots[:, None]).astype(jnp.int32)
    takes_int = takes.astype(jnp.int32)
    rank = jnp.where(
        takes,
        jnp.sum(before_me * takes_int[None, :], axis=1),
        jnp.sum(takes_int) + jnp.sum(before_me * (1 - takes_int)[None, :], axis=1),
    )
    wanted = jnp.minimum(spots, number - 1)
    order = jnp.sum(jnp.where(rank[None, :] == wanted[:, None], spots[None, :], 0), axis=1)
    order = jnp.concatenate([order, number[None]]).astype(jnp.int32)

    def constant(table):
        return pl.BlockSpec(table.shape, lambda i, g, *_: (0, 0))

    def page(i, g, scal, order):
        return (order[g], i, 0, 0)

    rest = SHARED_C - SHARED_D
    c6, c6_rest, ahead_row, d6, d6_self = values[:5]
    operands = [c6, c6, c6_rest, c6_rest, ahead_row, d6, d6_self]
    following = lambda i: jnp.minimum((i + 1) // 2, half_rows - 1)
    in_specs = [
        rest_spec(SHARED_D, lambda i: i // 2),
        rest_spec(SHARED_D, following),
        rest_spec(rest, lambda i: i // 2),
        rest_spec(rest, following),
        rest_spec(SHARED_C, lambda i: 0),
        rest_spec(SHARED_D, lambda i: i // 2),
        rest_spec(rest, lambda i: i // 2),
    ]
    aliases = {}
    if not fine:
        c5, c5_low, c5_high, s5_self = values[5:]
        operands += [c5[slot] for slot in SLOTS] + [c5_low, c5_high, s5_self]
        in_specs += [
            pl.BlockSpec((SHARED_D, 1, QR, HALF_LANES), lambda i, g, *_: (0, i, 0, 0))
        ] * 8 + [
            rest_spec(rest, lambda i: jnp.minimum(i, half_rows - 1)),
            rest_spec(rest, lambda i: jnp.maximum(i - half_rows, 0)),
            line_spec(lambda i: i),
        ]
        c4 = jnp.stack([c5[slot][SHARED_D] for slot in SLOTS])
        operands += [c4.reshape((2, 2, 2) + c4.shape[1:]), before]
        in_specs += [line_spec(lambda i: i), pl.BlockSpec(memory_space=pl.ANY)]
        aliases = {2 + len(operands) - 1: 0}
    return pl.pallas_call(
        lambda *refs: backward_kernel(fine, rows_here, count, *refs),
        grid_spec=pltpu.PrefetchScalarGridSpec(
            num_scalar_prefetch=2,
            grid=(rows_here, count),
            in_specs=in_specs + [constant(table) for table in ordered],
            out_specs=pl.BlockSpec((1, 1, N2, N3 * N4), page),
            scratch_shapes=[
                pltpu.VMEM((4, GROUPS, HB + QR, TILE), jnp.float32),
                pltpu.VMEM((4, GROUPS, HB, TILE), jnp.float32),
                pltpu.VMEM((GROUPS, N2, TILE), jnp.float32),
                pltpu.VMEM((GROUPS, N2, 12 * TILE), jnp.bfloat16),
            ],
        ),
        out_shape=jax.ShapeDtypeStruct((count, rows_here, N2, N3 * N4), jnp.float32),
        input_output_aliases=aliases,
        compiler_params=pltpu.CompilerParams(vmem_limit_bytes=60 * 2**20),
        cost_estimate=pl.CostEstimate(
            flops=10**10, bytes_accessed=60 * 2**20, transcendentals=0
        ),
        name="join_fine" if fine else "join_coarse",
    )(scal, order, *operands, *ordered)


def stack_slots(pieces):
    return jnp.stack(
        [
            jnp.stack([jnp.stack([pieces[h, sx, sy] for sy in range(2)]) for sx in range(2)])
            for h in range(2)
        ]
    )


def exchange(value, axis, domains):
    dom_count = lax.axis_size("dom")
    pairs = []
    for x in range(2):
        for y in range(2):
            other = (1 - x, y) if axis == "half" else (x, 1 - y)
            for d in range(domains):
                pairs.append(
                    ((x * 2 + y) * dom_count + d, (other[0] * 2 + other[1]) * dom_count + d)
                )
    return lax.ppermute(value, ("half", "grid", "dom"), pairs)


def reduce_quarter(pieces, domains):
    reduced = []
    for h in range(2):
        first, second = (("half", "grid"), ("grid", "half"))[h]
        far = lambda a, b: pieces[(h, a, b) if h == 0 else (h, b, a)]
        onward = exchange(far(1, 1), first, domains)
        nearby = exchange(far(1, 0), first, domains)
        onward = far(0, 1) + onward
        nearby = far(0, 0) + nearby
        reduced.append(nearby + exchange(onward, second, domains))
    return jnp.stack(reduced)


def gather_quarters(own, domains):
    pieces = {}
    for h in range(2):
        first, second = (("half", "grid"), ("grid", "half"))[h]
        place = lambda a, b: (h, a, b) if h == 0 else (h, b, a)
        pieces[place(0, 0)] = own[h]
        pieces[place(0, 1)] = exchange(own[h], second, domains)
        pieces[place(1, 0)] = exchange(own[h], first, domains)
        pieces[place(1, 1)] = exchange(pieces[place(0, 1)], first, domains)
    return pieces


def rows_up(value, sources):
    half_rows = value.shape[-3] // 2
    low = lax.ppermute(value[..., :half_rows, :, :], "dom", [(d, 2 * d) for d in range(sources)])
    high = lax.ppermute(
        value[..., half_rows:, :, :], "dom", [(d, 2 * d + 1) for d in range(sources)]
    )
    return low + high


def rows_down(value):
    targets = lax.axis_size("dom") // 2
    low = lax.ppermute(value, "dom", [(2 * d, d) for d in range(targets)])
    high = lax.ppermute(value, "dom", [(2 * d + 1, d) for d in range(targets)])
    return jnp.concatenate([low, high], axis=-3)


def next_row(value, devices):
    return lax.ppermute(
        value[..., :1, :, :], "dom", [((d + 1) % devices, d) for d in range(devices)]
    )


def per_device(grids, levels):
    count, rows_here = grids.shape[:2]
    half_rows = rows_here // 2
    half_size = lax.axis_size("half")
    grid_size = lax.axis_size("grid")
    dom_size = lax.axis_size("dom")
    square = half_size == 2 and grid_size == 2
    group = lax.axis_index("half") * grid_size + lax.axis_index("grid")
    weights = combination_weights(levels).astype(jnp.float32)
    lowest = jnp.array(
        [LEV1 - SPANS[0], LEV2 - SPANS[1], LEV3 - SPANS[2], LEV4 - SPANS[3]], dtype=jnp.int32
    )
    offsets = levels - lowest[None, :]
    own_offsets = lax.dynamic_slice_in_dim(offsets, group * count, count, 0)
    own_weights = lax.dynamic_slice_in_dim(weights, group * count, count, 0)
    zero = jnp.zeros((), jnp.int32)
    place = jnp.stack(
        [
            lax.axis_index("half") if square else zero,
            lax.axis_index("grid") if square else zero,
            lax.axis_index("dom") * rows_here,
        ]
    ).astype(jnp.int32)
    scal = jnp.concatenate([own_offsets.reshape(-1), place])
    sources = dom_size // 2
    quarter_devices = dom_size // 4
    s4 = coarsest(grids, scal, own_weights)[:, :, :, None]
    ahead = next_row(s4, quarter_devices)
    longer = jnp.concatenate([s4, ahead], axis=-3)
    mids = 0.5 * (longer[..., :-1, :, :] + longer[..., 1:, :, :])
    spread = jnp.stack([s4, mids], axis=-3).reshape(
        s4.shape[:-3] + (2 * rows_here,) + s4.shape[-2:]
    )
    spread = rows_up(spread, quarter_devices)
    coarsest_rows = rows_up(spread, sources)

    coarse_parts = forward(False, grids, scal, own_weights)
    s5 = dict(zip(SLOTS, coarse_parts[:8]))
    s5_low, s5_high, s5_self = coarse_parts[8:]
    fine_parts = forward(True, grids, scal, own_weights)
    e6 = dict(zip(SLOTS, fine_parts[:8]))
    d6 = dict(zip(SLOTS, fine_parts[8:16]))
    e6_rest, d6_self = fine_parts[16:]

    from_low = lax.ppermute(s5_low, "dom", [(d, 2 * d) for d in range(sources)])
    from_high = lax.ppermute(s5_high, "dom", [(d, 2 * d + 1) for d in range(sources)])
    c6_rest = e6_rest + from_low + from_high
    firsts = jnp.concatenate(
        [stack_slots({slot: e6[slot][:, :1] for slot in SLOTS}), e6_rest[..., :1, :, :]], axis=3
    )
    e6_ahead = next_row(firsts, dom_size)
    d6_self = d6_self.at[..., -1:, :, :].add(-0.5 * e6_ahead[:, :, :, SHARED_D:])
    d6 = {
        slot: d6[slot].at[:, -1:].add(-0.5 * e6_ahead[slot][:SHARED_D]) for slot in SLOTS
    }

    e6 = {slot: e6[slot].at[:1].add(coarsest_rows[slot]) for slot in SLOTS}

    if square:
        s5_own = reduce_quarter(s5, sources)
        d6_own = reduce_quarter(d6, dom_size)
        e6_own = reduce_quarter(e6, dom_size)
        rest_own = reduce_quarter({slot: c6_rest[slot] for slot in SLOTS}, dom_size)
    else:
        s5_own, e6_own, d6_own, rest_own = lax.psum(
            (stack_slots(s5), stack_slots(e6), stack_slots(d6), c6_rest), ("half", "grid")
        )
    c6_own = e6_own + rows_up(s5_own, sources)
    c5_own = rows_down(c6_own)
    if half_rows > 1:
        pieces = [
            lax.ppermute(
                c6_own[..., :1, ::2, :, :], "dom", [(4 * d + r, d) for d in range(quarter_devices)]
            )
            for r in range(4)
        ]
    else:
        pieces = [
            lax.ppermute(
                c6_own[..., :1, :, :, :], "dom", [(4 * d + r, d) for d in range(quarter_devices)]
            )
            for r in (0, 2)
        ]
    c4_own = jnp.concatenate(pieces, axis=-3)
    c5_own = jnp.concatenate([c5_own, c4_own], axis=-4)
    ahead_own = next_row(
        jnp.concatenate([c6_own[..., :1, :, :], rest_own[..., :1, :, :]], axis=-4), dom_size
    )
    if square:
        d6 = stack_slots(gather_quarters(d6_own, dom_size))
        c6_rest = stack_slots(gather_quarters(rest_own, dom_size))
        c6 = stack_slots(gather_quarters(c6_own, dom_size))
        ahead_row = stack_slots(gather_quarters(ahead_own, dom_size))
        c5 = gather_quarters(c5_own, sources)
    else:
        c6, d6, c6_rest, ahead_row = c6_own, d6_own, rest_own, ahead_own
        c5 = {slot: c5_own[slot] for slot in SLOTS}
    c5_low = lax.ppermute(c6_rest, "dom", [(2 * d, d) for d in range(sources)])
    c5_high = lax.ppermute(c6_rest, "dom", [(2 * d + 1, d) for d in range(sources)])
    values = [c6, c6_rest, ahead_row, d6, d6_self]
    written = backward(True, count, scal, rows_here, values)
    values += [c5, c5_low, c5_high, s5_self]
    return backward(False, count, scal, rows_here, values, written)


def solution(mesh):
    return jax.shard_map(
        per_device,
        mesh=mesh,
        in_specs=(P(("half", "grid"), "dom", None, None), P()),
        out_specs=P(("half", "grid"), "dom", None, None),
        check_vma=False,
    )
```

profile of v0, /device:TPU:0, one launch (start us, length us, event | category | flops | bytes accessed | tf_op | source)
XLA Modules:
  0.0 477.6 jit_solution(16705704926770877028)
XLA Ops:
  5.8 17.0 %split_coarsest.1 = f32[2,2,2,8,8,512]{5,4,3,2,1,0:T(8,128)} custom-call(s32[19]{0:T(128)} %pad_add_fusion.refs_0_, f32[4]{0:T(128)} %dynamic_slice.7.refs_2_.refs_1_, f32[4,8,64,4096]{3,2,1,0:T(8,128)} %refs_3_.4, bf16[256,128]{1,0:T(8,128)(2,1)} %constant.432.clone.refs_4_.refs_3_), custom_call_target="tpu_custom_call" | custom-call | flops 100000000 | bytes 4194304 | tf_op jit(solution)/shard_map/split_coarsest/pallas_call | solution.py:362
  27.6 31.0 %split_fine.1 = (f32[4,4,8,512]{3,2,1,0:T(8,128)}, f32[4,4,8,512]{3,2,1,0:T(8,128)}, f32[4,4,8,512]{3,2,1,0:T(8,128)}, f32[4,4,8,512]{3,2,1,0:T(8,128)}, f32[4,4...) custom-call(s32[19]{0:T(128)} %pad_add_fusion.refs_0_, ...), custom_call_target="tpu_custom_call" | custom-call | flops 10000000000 | bytes 62914560 | tf_op jit(solution)/shard_map/split_fine/pallas_call | solution.py:303
  64.2 33.4 %split_coarse.1 = (f32[4,8,8,512]{3,2,1,0:T(8,128)}, f32[4,8,8,512]{3,2,1,0:T(8,128)}, f32[4,8,8,512]{3,2,1,0:T(8,128)}, f32[4,8,8,512]{3,2,1,0:T(8,128)}, f32[4...) custom-call(s32[19]{0:T(128)} %pad_add_fusion.refs_0_, ...), custom_call_target="tpu_custom_call" | custom-call | flops 10000000000 | bytes 62914560 | tf_op jit(solution)/shard_map/split_coarse/pallas_call | solution.py:303
  99.5 3.9 collective-permute-start.12
  109.9 3.9 collective-permute-start.15
  114.7 10.6 %collective-permute-done.12 = f32[4,8,8,512]{3,2,1,0:T(8,128)} collective-permute-done((f32[4,8,8,512]{3,2,1,0:T(8,128)}, f32[4,8,8,512]{3,2,1,0:T(8,128)}, u32[]{:S(2)}, u32[]{:S(2)}) %collective-permute-start.12) | collective-permute-done | bytes 524320 | tf_op jit(solution)/shard_map/ppermute | solution.py:607
  140.6 6.0 %collective-permute-done.13 = f32[4,8,8,512]{3,2,1,0:T(8,128)S(1)} collective-permute-done((f32[4,8,8,512]{3,2,1,0:T(8,128)S(1)}, f32[4,8,8,512]{3,2,1,0:T(8,128)S(1)}, u32[]{:S(2)}, u32[]{:S(2)}) %collective-permute-start.13) | collective-permute-done | bytes 524320 | tf_op jit(solution)/shard_map/ppermute | solution.py:607
  149.5 3.5 collective-permute-done.16
  157.0 5.1 %collective-permute-done.54 = f32[4,4,8,512]{3,2,1,0:T(8,128)S(1)} collective-permute-done((f32[4,4,8,512]{3,2,1,0:T(8,128)S(1)}, f32[4,4,8,512]{3,2,1,0:T(8,128)S(1)}, u32[]{:S(2)}, u32[]{:S(2)}) %collective-permute-start.54) | collective-permute-done | bytes 262176 | tf_op jit(solution)/shard_map/ppermute | solution.py:607
  166.9 5.8 %collective-permute-done.55 = f32[4,4,8,512]{3,2,1,0:T(8,128)S(1)} collective-permute-done((f32[4,4,8,512]{3,2,1,0:T(8,128)S(1)}, f32[4,4,8,512]{3,2,1,0:T(8,128)S(1)}, u32[]{:S(2)}, u32[]{:S(2)}) %collective-permute-start.55) | collective-permute-done | bytes 262176 | tf_op jit(solution)/shard_map/ppermute | solution.py:607
  186.4 4.1 collective-permute-done.28
  196.9 3.6 collective-permute-start.29
  201.3 6.8 %collective-permute-done.29 = f32[3,4,8,512]{3,2,1,0:T(8,128)S(1)} collective-permute-done((f32[3,4,8,512]{3,2,1,0:T(8,128)S(1)}, f32[3,4,8,512]{3,2,1,0:T(8,128)S(1)}, u32[]{:S(2)}, u32[]{:S(2)}) %collective-permute-start.29) | collective-permute-done | bytes 196640 | tf_op jit(solution)/shard_map/ppermute | solution.py:607
  211.6 11.3 %collective-permute-start.18 = (f32[2,4,4,8,512]{4,3,2,1,0:T(8,128)S(1)}, f32[2,4,4,8,512]{4,3,2,1,0:T(8,128)S(1)}, u32[]{:S(2)}, u32[]{:S(2)}) collective-permute-start(f32[2,4,4,8,512]{4,3,2,1,0:T(8,128)S(1)} %get-tuple-element.279), channel_id=1, source_target_pairs={{0,1},{1,3},{2,5},{3,7},{8,9},{9,11},{10,13},{11,15},{16,17},{17,1... | collective-permute-start | bytes 1572872 | tf_op jit(solution)/shard_map/ppermute | solution.py:638
  242.3 42.7 %collective-permute-done.62 = f32[2,1,2,8,512]{4,3,2,1,0:T(8,128)S(1)} collective-permute-done((f32[2,1,2,8,512]{4,3,2,1,0:T(8,128)S(1)}, f32[2,1,2,8,512]{4,3,2,1,0:T(8,128)S(1)}, u32[]{:S(2)}, u32[]{:S(2)}) %collective-permute-start.62) | collective-permute-done | bytes 65568 | tf_op jit(solution)/shard_map/ppermute | solution.py:728
  286.3 4.8 %collective-permute-done.63 = f32[2,1,2,8,512]{4,3,2,1,0:T(8,128)S(1)} collective-permute-done((f32[2,1,2,8,512]{4,3,2,1,0:T(8,128)S(1)}, f32[2,1,2,8,512]{4,3,2,1,0:T(8,128)S(1)}, u32[]{:S(2)}, u32[]{:S(2)}) %collective-permute-start.63) | collective-permute-done | bytes 65568 | tf_op jit(solution)/shard_map/ppermute | solution.py:728
  292.5 4.3 collective-permute-done.64
  298.7 5.3 %collective-permute-start.39 = (f32[2,7,1,8,512]{4,3,2,1,0:T(8,128)S(1)}, f32[2,7,1,8,512]{4,3,2,1,0:T(8,128)S(1)}, u32[]{:S(2)}, u32[]{:S(2)}) collective-permute-start(f32[2,7,1,8,512]{4,3,2,1,0:T(8,128)S(1)} %fusion.6), channel_id=1, source_target_pairs={{1,0},{2,1},{3,2},{4,3},{5,4},{6,5},{7,6},{0,7},{9,8},{10,9},{11,1... | collective-permute-start | bytes 688136 | tf_op jit(solution)/shard_map/ppermute | solution.py:652
  310.4 3.0 collective-permute-done.19
  314.5 3.4 collective-permute-done.22
  323.4 4.0 collective-permute-done.40
  330.2 2.7 collective-permute-done.43
  335.5 3.3 collective-permute-done.42
  347.2 2.9 collective-permute-start.65
  354.9 3.8 collective-permute-start.66
  360.8 5.8 %collective-permute-done.65.refs_10_ = f32[5,8,8,512]{3,2,1,0:T(8,128)S(1)} collective-permute-done((f32[5,8,8,512]{3,2,1,0:T(8,128)S(1)}, f32[5,8,8,512]{3,2,1,0:T(8,128)S(1)}, u32[]{:S(2)}, u32[]{:S(2)}) %collective-permute-start.65) | collective-permute-done | bytes 655392 | tf_op jit(solution)/shard_map/ppermute | solution.py:607
  366.6 4.1 collective-permute-start.67
  370.6 32.4 %join_fine.1.refs_21_ = f32[4,8,64,4096]{3,2,1,0:T(8,128)} custom-call(s32[19]{0:T(128)} %pad_add_fusion.refs_0_, s32[5]{0:T(128)} %pad_add_fusion.2.refs_1_, f32[2,2,2,4,4,8,512]{6,5,4,3,2,1,0:T(8,128)} %pad_maximum_fusion.1.refs_2_.refs_3_, f32[2,2,2,4,4,8,512]{6,5,4,3,2,1,0:T(8,128)} %pad_maximum_fusion.1.refs_2_.refs_3_, ...), custom_call_target="tpu_custom_call" | custom-call | flops 10000000000 | bytes 62914560 | tf_op jit(solution)/shard_map/join_fine/pallas_call | solution.py:564
  405.6 3.9 collective-permute-start.70
  413.4 9.8 %collective-permute-done.68.refs_14_ = f32[5,8,8,512]{3,2,1,0:T(8,128)S(1)} collective-permute-done((f32[5,8,8,512]{3,2,1,0:T(8,128)S(1)}, f32[5,8,8,512]{3,2,1,0:T(8,128)S(1)}, u32[]{:S(2)}, u32[]{:S(2)}) %collective-permute-start.68) | collective-permute-done | bytes 655392 | tf_op jit(solution)/shard_map/ppermute | solution.py:607
  425.5 10.9 %collective-permute-done.70.refs_16_ = f32[5,8,8,512]{3,2,1,0:T(8,128)S(1)} collective-permute-done((f32[5,8,8,512]{3,2,1,0:T(8,128)}, f32[5,8,8,512]{3,2,1,0:T(8,128)S(1)}, u32[]{:S(2)}, u32[]{:S(2)}) %collective-permute-start.70) | collective-permute-done | bytes 655392 | tf_op jit(solution)/shard_map/ppermute | solution.py:607
  437.3 40.1 %join_coarse.1 = f32[4,8,64,4096]{3,2,1,0:T(8,128)} custom-call(s32[19]{0:T(128)} %pad_add_fusion.refs_0_, s32[5]{0:T(128)} %pad_add_fusion.1.refs_1_, f32[2,2,2,4,4,8,512]{6,5,4,3,2,1,0:T(8,128)} %pad_maximum_fusion.1.refs_2_.refs_3_, f32[2,2,2,4,4,8,512]{6,5,4,3,2,1,0:T(8,128)} %pad_maximum_fusion.1.refs_2_.refs_3_, ...), custom_call_target="tpu_custom_call", output_to_operand_aliasing={{}: (21, {})} | custom-call | flops 10000000000 | bytes 62914560 | tf_op jit(solution)/shard_map/join_coarse/pallas_call | solution.py:564
  (309 shorter events, 141.4 us)
Async XLA Ops:
  24.4 85.5 %collective-permute-start = (f32[2,2,2,1,1,8,512]{6,5,4,2,1,0,3:T(8,128)}, f32[2,2,2,1,1,8,512]{6,5,4,2,1,0,3:T(8,128)S(1)}, u32[]{:S(2)}, u32[]{:S(2)}) collective-permute-start(f32[2,2,2,1,1,8,512]{6,5,4,2,1,0,3:T(8,128)} %slice.819), channel_id=1, source_target_pairs={{1,0},{0,1},{9,8},{8,9},{17,16},{16,17},{25,24},{24,25}} | collective-permute-start | bytes 393224 | tf_op jit(solution)/shard_map/ppermute | solution.py:652
  63.4 67.8 %collective-permute-start.46 = (f32[2,2,2,7,1,8,512]{6,5,4,3,2,1,0:T(8,128)S(1)}, f32[2,2,2,7,1,8,512]{6,5,4,3,2,1,0:T(8,128)S(1)}, u32[]{:S(2)}, u32[]{:S(2)}) collective-permute-start(f32[2,2,2,7,1,8,512]{6,5,4,3,2,1,0:T(8,128)S(1)} %pad_maximum_fusion.6), channel_id=1, source_target_pairs={{1,0},{2,1},{3,2},{4,3},{5,4},{6,5},{7,6},{0,7},{9,8},{10,9},{11,1... | collective-permute-start | bytes 2752520 | tf_op jit(solution)/shard_map/ppermute | solution.py:652
  97.5 39.9 %collective-permute-start.11 = (f32[4,8,8,512]{3,2,1,0:T(8,128)}, f32[4,8,8,512]{3,2,1,0:T(8,128)}, u32[]{:S(2)}, u32[]{:S(2)}) collective-permute-start(f32[4,8,8,512]{3,2,1,0:T(8,128)} %get-tuple-element.247), channel_id=1, source_target_pairs={{0,16},{1,17},{2,18},{3,19},{8,24},{9,25},{10,26},{11,27},{16,0},{... | collective-permute-start | bytes 1572872 | tf_op jit(solution)/shard_map/ppermute | solution.py:607
  99.5 25.8 %collective-permute-start.12 = (f32[4,8,8,512]{3,2,1,0:T(8,128)}, f32[4,8,8,512]{3,2,1,0:T(8,128)}, u32[]{:S(2)}, u32[]{:S(2)}) collective-permute-start(f32[4,8,8,512]{3,2,1,0:T(8,128)} %get-tuple-element.249), channel_id=1, source_target_pairs={{0,16},{1,17},{2,18},{3,19},{8,24},{9,25},{10,26},{11,27},{16,0},{... | collective-permute-start | bytes 1572872 | tf_op jit(solution)/shard_map/ppermute | solution.py:607
  103.4 36.4 %collective-permute-start.14 = (f32[4,8,8,512]{3,2,1,0:T(8,128)}, f32[4,8,8,512]{3,2,1,0:T(8,128)}, u32[]{:S(2)}, u32[]{:S(2)}) collective-permute-start(f32[4,8,8,512]{3,2,1,0:T(8,128)} %get-tuple-element.251), channel_id=1, source_target_pairs={{0,8},{1,9},{2,10},{3,11},{8,0},{9,1},{10,2},{11,3},{16,24},{17,25... | collective-permute-start | bytes 1572872 | tf_op jit(solution)/shard_map/ppermute | solution.py:607
  109.9 20.6 %collective-permute-start.15 = (f32[4,8,8,512]{3,2,1,0:T(8,128)}, f32[4,8,8,512]{3,2,1,0:T(8,128)S(1)}, u32[]{:S(2)}, u32[]{:S(2)}) collective-permute-start(f32[4,8,8,512]{3,2,1,0:T(8,128)} %get-tuple-element.253), channel_id=1, source_target_pairs={{0,8},{1,9},{2,10},{3,11},{8,0},{9,1},{10,2},{11,3},{16,24},{17,25... | collective-permute-start | bytes 1572872 | tf_op jit(solution)/shard_map/ppermute | solution.py:607
  125.3 29.1 %collective-permute-start.2 = (f32[2,2,2,1,8,8,512]{6,5,4,3,2,1,0:T(8,128)S(1)}, f32[2,2,2,1,8,8,512]{6,5,4,3,2,1,0:T(8,128)S(1)}, u32[]{:S(2)}, u32[]{:S(2)}) collective-permute-start(f32[2,2,2,1,8,8,512]{6,5,4,3,2,1,0:T(8,128)S(1)} %get-tuple-element.269), channel_id=1, source_target_pairs={{0,1},{1,3},{8,9},{9,11},{16,17},{17,19},{24,25},{25,27}} | collective-permute-start | bytes 3145736 | tf_op jit(solution)/shard_map/ppermute | solution.py:638
  130.5 24.5 %collective-permute-start.1 = (f32[2,2,2,1,8,8,512]{6,5,4,3,2,1,0:T(8,128)S(1)}, f32[2,2,2,1,8,8,512]{6,5,4,3,2,1,0:T(8,128)S(1)}, u32[]{:S(2)}, u32[]{:S(2)}) collective-permute-start(f32[2,2,2,1,8,8,512]{6,5,4,3,2,1,0:T(8,128)S(1)} %get-tuple-element.270), channel_id=1, source_target_pairs={{0,0},{1,2},{8,8},{9,10},{16,16},{17,18},{24,24},{25,26}} | collective-permute-start | bytes 3145736 | tf_op jit(solution)/shard_map/ppermute | solution.py:637
  139.8 35.8 %collective-permute-start.25 = (f32[2,2,2,3,4,8,512]{6,5,4,3,2,1,0:T(8,128)S(1)}, f32[2,2,2,3,4,8,512]{6,5,4,3,2,1,0:T(8,128)S(1)}, u32[]{:S(2)}, u32[]{:S(2)}) collective-permute-start(f32[2,2,2,3,4,8,512]{6,5,4,3,2,1,0:T(8,128)S(1)} %copy-done.29), channel_id=1, source_target_pairs={{0,0},{1,2},{2,4},{3,6},{8,8},{9,10},{10,12},{11,14},{16,16},{17,1... | collective-permute-start | bytes 4718600 | tf_op jit(solution)/shard_map/ppermute | solution.py:701
  146.7 30.3 %collective-permute-start.26 = (f32[2,2,2,3,4,8,512]{6,5,4,3,2,1,0:T(8,128)S(1)}, f32[2,2,2,3,4,8,512]{6,5,4,3,2,1,0:T(8,128)S(1)}, u32[]{:S(2)}, u32[]{:S(2)}) collective-permute-start(f32[2,2,2,3,4,8,512]{6,5,4,3,2,1,0:T(8,128)S(1)} %copy-done.28), channel_id=1, source_target_pairs={{0,1},{1,3},{2,5},{3,7},{8,9},{9,11},{10,13},{11,15},{16,17},{17,1... | collective-permute-start | bytes 4718600 | tf_op jit(solution)/shard_map/ppermute | solution.py:702
  176.9 18.2 %collective-permute-start.51 = (f32[4,4,8,512]{3,2,1,0:T(8,128)S(1)}, f32[4,4,8,512]{3,2,1,0:T(8,128)S(1)}, u32[]{:S(2)}, u32[]{:S(2)}) collective-permute-start(f32[4,4,8,512]{3,2,1,0:T(8,128)S(1)} %add_add_fusion.2), channel_id=1, source_target_pairs={{0,16},{1,17},{2,18},{3,19},{4,20},{5,21},{6,22},{7,23},{8,24},{9,... | collective-permute-start | bytes 786440 | tf_op jit(solution)/shard_map/ppermute | solution.py:607
  180.0 20.7 %collective-permute-start.27 = (f32[3,4,8,512]{3,2,1,0:T(8,128)S(1)}, f32[3,4,8,512]{3,2,1,0:T(8,128)S(1)}, u32[]{:S(2)}, u32[]{:S(2)}) collective-permute-start(f32[3,4,8,512]{3,2,1,0:T(8,128)S(1)} %get-tuple-element.273), channel_id=1, source_target_pairs={{0,16},{1,17},{2,18},{3,19},{4,20},{5,21},{6,22},{7,23},{8,24},{9,... | collective-permute-start | bytes 589832 | tf_op jit(solution)/shard_map/ppermute | solution.py:607
  192.6 31.1 %collective-permute-start.33 = (f32[3,4,8,512]{3,2,1,0:T(8,128)S(1)}, f32[3,4,8,512]{3,2,1,0:T(8,128)S(1)}, u32[]{:S(2)}, u32[]{:S(2)}) collective-permute-start(f32[3,4,8,512]{3,2,1,0:T(8,128)S(1)} %get-tuple-element.275), channel_id=1, source_target_pairs={{0,8},{1,9},{2,10},{3,11},{4,12},{5,13},{6,14},{7,15},{8,0},{9,1},... | collective-permute-start | bytes 589832 | tf_op jit(solution)/shard_map/ppermute | solution.py:607
  200.6 25.9 %collective-permute-start.8 = (f32[4,4,8,512]{3,2,1,0:T(8,128)S(1)}, f32[4,4,8,512]{3,2,1,0:T(8,128)S(1)}, u32[]{:S(2)}, u32[]{:S(2)}) collective-permute-start(f32[4,4,8,512]{3,2,1,0:T(8,128)S(1)} %get-tuple-element.298), channel_id=1, source_target_pairs={{0,8},{1,9},{2,10},{3,11},{4,12},{5,13},{6,14},{7,15},{8,0},{9,1},... | collective-permute-start | bytes 786440 | tf_op jit(solution)/shard_map/ppermute | solution.py:607
  200.7 22.2 %collective-permute-start.6 = (f32[4,4,8,512]{3,2,1,0:T(8,128)S(1)}, f32[4,4,8,512]{3,2,1,0:T(8,128)S(1)}, u32[]{:S(2)}, u32[]{:S(2)}) collective-permute-start(f32[4,4,8,512]{3,2,1,0:T(8,128)S(1)} %get-tuple-element.300), channel_id=1, source_target_pairs={{0,16},{1,17},{2,18},{3,19},{4,20},{5,21},{6,22},{7,23},{8,24},{9,... | collective-permute-start | bytes 786440 | tf_op jit(solution)/shard_map/ppermute | solution.py:607
  211.6 27.1 %collective-permute-start.18 = (f32[2,4,4,8,512]{4,3,2,1,0:T(8,128)S(1)}, f32[2,4,4,8,512]{4,3,2,1,0:T(8,128)S(1)}, u32[]{:S(2)}, u32[]{:S(2)}) collective-permute-start(f32[2,4,4,8,512]{4,3,2,1,0:T(8,128)S(1)} %get-tuple-element.279), channel_id=1, source_target_pairs={{0,1},{1,3},{2,5},{3,7},{8,9},{9,11},{10,13},{11,15},{16,17},{17,1... | collective-permute-start | bytes 1572872 | tf_op jit(solution)/shard_map/ppermute | solution.py:638
  232.2 71.8 %collective-permute-start.31 = (f32[3,4,8,512]{3,2,1,0:T(8,128)S(1)}, f32[3,4,8,512]{3,2,1,0:T(8,128)S(1)}, u32[]{:S(2)}, u32[]{:S(2)}) collective-permute-start(f32[3,4,8,512]{3,2,1,0:T(8,128)S(1)} %get-tuple-element.271), channel_id=1, source_target_pairs={{0,16},{1,17},{2,18},{3,19},{4,20},{5,21},{6,22},{7,23},{8,24},{9,... | collective-permute-start | bytes 589832 | tf_op jit(solution)/shard_map/ppermute | solution.py:607
  233.7 75.0 %collective-permute-start.37 = (f32[3,4,8,512]{3,2,1,0:T(8,128)S(1)}, f32[3,4,8,512]{3,2,1,0:T(8,128)S(1)}, u32[]{:S(2)}, u32[]{:S(2)}) collective-permute-start(f32[3,4,8,512]{3,2,1,0:T(8,128)S(1)} %fusion.9), channel_id=1, source_target_pairs={{0,16},{1,17},{2,18},{3,19},{4,20},{5,21},{6,22},{7,23},{8,24},{9,... | collective-permute-start | bytes 589832 | tf_op jit(solution)/shard_map/ppermute | solution.py:607
  237.0 61.7 %collective-permute-start.36 = (f32[3,4,8,512]{3,2,1,0:T(8,128)S(1)}, f32[3,4,8,512]{3,2,1,0:T(8,128)S(1)}, u32[]{:S(2)}, u32[]{:S(2)}) collective-permute-start(f32[3,4,8,512]{3,2,1,0:T(8,128)S(1)} %fusion.9), channel_id=1, source_target_pairs={{0,8},{1,9},{2,10},{3,11},{4,12},{5,13},{6,14},{7,15},{8,0},{9,1},... | collective-permute-start | bytes 589832 | tf_op jit(solution)/shard_map/ppermute | solution.py:607
  238.6 66.2 %collective-permute-start.32 = (f32[3,4,8,512]{3,2,1,0:T(8,128)S(1)}, f32[3,4,8,512]{3,2,1,0:T(8,128)S(1)}, u32[]{:S(2)}, u32[]{:S(2)}) collective-permute-start(f32[3,4,8,512]{3,2,1,0:T(8,128)S(1)} %collective-permute-done.30), channel_id=1, source_target_pairs={{0,16},{1,17},{2,18},{3,19},{4,20},{5,21},{6,22},{7,23},{8,24},{9,... | collective-permute-start | bytes 589832 | tf_op jit(solution)/shard_map/ppermute | solution.py:607
  241.0 44.1 %collective-permute-start.62 = (f32[2,1,2,8,512]{4,3,2,1,0:T(8,128)S(1)}, f32[2,1,2,8,512]{4,3,2,1,0:T(8,128)S(1)}, u32[]{:S(2)}, u32[]{:S(2)}) collective-permute-start(f32[2,1,2,8,512]{4,3,2,1,0:T(8,128)S(1)} %slice.806), channel_id=1, source_target_pairs={{1,0},{5,1},{9,8},{13,9},{17,16},{21,17},{25,24},{29,25}} | collective-permute-start | bytes 196616 | tf_op jit(solution)/shard_map/ppermute | solution.py:728
  296.8 48.9 %collective-permute-start.60 = (f32[2,4,4,8,512]{4,3,2,1,0:T(8,128)S(1)}, f32[2,4,4,8,512]{4,3,2,1,0:T(8,128)S(1)}, u32[]{:S(2)}, u32[]{:S(2)}) collective-permute-start(f32[2,4,4,8,512]{4,3,2,1,0:T(8,128)S(1)} %maximum_add_fusion), channel_id=1, source_target_pairs={{1,0},{3,1},{5,2},{7,3},{9,8},{11,9},{13,10},{15,11},{17,16},{19,1... | collective-permute-start | bytes 1572872 | tf_op jit(solution)/shard_map/ppermute | solution.py:647
  304.1 42.8 %collective-permute-start.59 = (f32[2,4,4,8,512]{4,3,2,1,0:T(8,128)S(1)}, f32[2,4,4,8,512]{4,3,2,1,0:T(8,128)S(1)}, u32[]{:S(2)}, u32[]{:S(2)}) collective-permute-start(f32[2,4,4,8,512]{4,3,2,1,0:T(8,128)S(1)} %maximum_add_fusion), channel_id=1, source_target_pairs={{0,0},{2,1},{4,2},{6,3},{8,8},{10,9},{12,10},{14,11},{16,16},{18,1... | collective-permute-start | bytes 1572872 | tf_op jit(solution)/shard_map/ppermute | solution.py:646
  308.7 31.2 %collective-permute-start.23 = (f32[4,4,8,512]{3,2,1,0:T(8,128)S(1)}, f32[4,4,8,512]{3,2,1,0:T(8,128)S(1)}, u32[]{:S(2)}, u32[]{:S(2)}) collective-permute-start(f32[4,4,8,512]{3,2,1,0:T(8,128)S(1)} %get-tuple-element.293), channel_id=1, source_target_pairs={{0,16},{1,17},{2,18},{3,19},{4,20},{5,21},{6,22},{7,23},{8,24},{9,... | collective-permute-start | bytes 786440 | tf_op jit(solution)/shard_map/ppermute | solution.py:607
  345.6 91.5 %collective-permute-start.72 = (f32[2,2,2,3,4,8,512]{6,5,4,3,2,1,0:T(8,128)S(1)}, f32[2,2,2,3,4,8,512]{6,5,4,3,2,1,0:T(8,128)}, u32[]{:S(2)}, u32[]{:S(2)}) collective-permute-start(f32[2,2,2,3,4,8,512]{6,5,4,3,2,1,0:T(8,128)S(1)} %pad_maximum_fusion.3.refs_4_.refs_5_), channel_id=1, source_target_pairs={{1,0},{3,1},{5,2},{7,3},{9,8},{11,9},{13,10},{15,11},{17,16},{19,1... | collective-permute-start | bytes 4718600 | tf_op jit(solution)/shard_map/ppermute | solution.py:755
  347.2 19.3 %collective-permute-start.65 = (f32[5,8,8,512]{3,2,1,0:T(8,128)S(1)}, f32[5,8,8,512]{3,2,1,0:T(8,128)S(1)}, u32[]{:S(2)}, u32[]{:S(2)}) collective-permute-start(f32[5,8,8,512]{3,2,1,0:T(8,128)S(1)} %get-tuple-element.278.refs_9_), channel_id=1, source_target_pairs={{0,8},{1,9},{2,10},{3,11},{8,0},{9,1},{10,2},{11,3},{16,24},{17,25... | collective-permute-start | bytes 1966088 | tf_op jit(solution)/shard_map/ppermute | solution.py:607
  351.1 86.0 %collective-permute-start.71 = (f32[2,2,2,3,4,8,512]{6,5,4,3,2,1,0:T(8,128)S(1)}, f32[2,2,2,3,4,8,512]{6,5,4,3,2,1,0:T(8,128)}, u32[]{:S(2)}, u32[]{:S(2)}) collective-permute-start(f32[2,2,2,3,4,8,512]{6,5,4,3,2,1,0:T(8,128)S(1)} %pad_maximum_fusion.3.refs_4_.refs_5_), channel_id=1, source_target_pairs={{0,0},{2,1},{4,2},{6,3},{8,8},{10,9},{12,10},{14,11},{16,16},{18,1... | collective-permute-start | bytes 4718600 | tf_op jit(solution)/shard_map/ppermute | solution.py:754
  354.9 50.7 %collective-permute-start.66 = (f32[5,8,8,512]{3,2,1,0:T(8,128)S(1)}, f32[5,8,8,512]{3,2,1,0:T(8,128)}, u32[]{:S(2)}, u32[]{:S(2)}) collective-permute-start(f32[5,8,8,512]{3,2,1,0:T(8,128)S(1)} %get-tuple-element.278.refs_9_), channel_id=1, source_target_pairs={{0,16},{1,17},{2,18},{3,19},{8,24},{9,25},{10,26},{11,27},{16,0},{... | collective-permute-start | bytes 1966088 | tf_op jit(solution)/shard_map/ppermute | solution.py:607
  358.8 44.9 %collective-permute-start.69 = (f32[5,8,8,512]{3,2,1,0:T(8,128)S(1)}, f32[5,8,8,512]{3,2,1,0:T(8,128)}, u32[]{:S(2)}, u32[]{:S(2)}) collective-permute-start(f32[5,8,8,512]{3,2,1,0:T(8,128)S(1)} %get-tuple-element.277.refs_13_), channel_id=1, source_target_pairs={{0,16},{1,17},{2,18},{3,19},{8,24},{9,25},{10,26},{11,27},{16,0},{... | collective-permute-start | bytes 1966088 | tf_op jit(solution)/shard_map/ppermute | solution.py:607
  366.6 44.6 %collective-permute-start.67 = (f32[5,8,8,512]{3,2,1,0:T(8,128)S(1)}, f32[5,8,8,512]{3,2,1,0:T(8,128)}, u32[]{:S(2)}, u32[]{:S(2)}) collective-permute-start(f32[5,8,8,512]{3,2,1,0:T(8,128)S(1)} %collective-permute-done.65.refs_10_), channel_id=1, source_target_pairs={{0,16},{1,17},{2,18},{3,19},{8,24},{9,25},{10,26},{11,27},{16,0},{... | collective-permute-start | bytes 1966088 | tf_op jit(solution)/shard_map/ppermute | solution.py:607
  403.7 19.5 %collective-permute-start.68 = (f32[5,8,8,512]{3,2,1,0:T(8,128)S(1)}, f32[5,8,8,512]{3,2,1,0:T(8,128)S(1)}, u32[]{:S(2)}, u32[]{:S(2)}) collective-permute-start(f32[5,8,8,512]{3,2,1,0:T(8,128)S(1)} %get-tuple-element.277.refs_13_), channel_id=1, source_target_pairs={{0,8},{1,9},{2,10},{3,11},{8,0},{9,1},{10,2},{11,3},{16,24},{17,25... | collective-permute-start | bytes 1966088 | tf_op jit(solution)/shard_map/ppermute | solution.py:607
  405.6 30.8 %collective-permute-start.70 = (f32[5,8,8,512]{3,2,1,0:T(8,128)}, f32[5,8,8,512]{3,2,1,0:T(8,128)S(1)}, u32[]{:S(2)}, u32[]{:S(2)}) collective-permute-start(f32[5,8,8,512]{3,2,1,0:T(8,128)} %collective-permute-done.69.refs_15_), channel_id=1, source_target_pairs={{0,8},{1,9},{2,10},{3,11},{8,0},{9,1},{10,2},{11,3},{16,24},{17,25... | collective-permute-start | bytes 1966088 | tf_op jit(solution)/shard_map/ppermute | solution.py:607
  (71 other events, 741.1 us)
where the time goes:
time: 481 us; the launch traced here: 478 us
  waiting for transfers between devices  157 us (33%)
  Pallas kernels  154 us (32%)
  starting transfers between devices  123 us (26%)
  other arithmetic  23.1 us (5%)
  local copies, waits for them, and re-layouts  18.2 us (4%)
    ppermute x54, waiting for transfers between devices, exchange(): return lax.ppermute(value, ('half', 'grid', 'dom'), pairs)  104 us
    ppermute x54, starting transfers between devices, exchange(): return lax.ppermute(value, ('half', 'grid', 'dom'), pairs)  86.5 us
    pallas_call x2, Pallas kernels, backward(): pl.pallas_call(lambda *refs: backward_kernel(fine, rows_here, count, *ref...  72.5 us
    pallas_call x2, Pallas kernels, forward(): pl.pallas_call(lambda *refs: forward_kernel(fine, rows_here, count, *refs...  64.3 us
    ppermute x4, waiting for transfers between devices, per_device(): lax.ppermute(c6_own[..., :1, ::2, :, :], 'dom', [(4 * d + r, d) for d in...  51.9 us
    pallas_call x1, Pallas kernels, coarsest(): pl.pallas_call(lambda *refs: coarsest_kernel(count, *refs), grid_spec=plt...  17 us
    ppermute x3, starting transfers between devices, rows_up(): lax.ppermute(value[..., half_rows:, :, :], 'dom', [(d, 2 * d + 1) for d i...  14.2 us
  transfers between devices with their start and end apart: 73, of which 29 were waited for; matrix products, arithmetic and copies ran while one was open for 7% of the time, Pallas kernels for 20%

commit v1 on v0

--- a/solution.py
+++ b/solution.py
@@ -126,9 +126,9 @@
     return tuple(scal[4 * g + axis] for axis in range(4))
 
 
-def forward_kernel(fine, rows_here, count, scal, fetch, weight, x_ref, *refs):
+def forward_kernel(rows_here, count, scal, fetch, weight, x_ref, *refs):
     tables = dict(zip(CASES, refs[:4]))
-    outs = refs[4:-2]
+    outs = refs[5:-2]
     xb, yb = refs[-2:]
     half_rows = rows_here // 2
     i = pl.program_id(0)
@@ -140,7 +140,7 @@
     odd = lax.rem(i, 2) == 1
     even = lax.rem(i, 2) == 0
     active = row < (N1 // 4) * (1 << level)
-    active = active & (level == (2 if fine else 1))
+    active = active & (level > 0)
 
     def clear(wanted, *targets):
         @pl.when((g == 0) & wanted)
@@ -148,38 +148,36 @@
             for target in targets:
                 target[...] = jnp.zeros_like(target)
 
-    if fine:
-        e6 = dict(zip(SLOTS, outs[:8]))
-        d6 = dict(zip(SLOTS, outs[8:16]))
-        e6_rest, d6_self = outs[16:]
-        clear(even, *outs[:8], e6_rest)
-        clear(odd, *outs[8:16], d6_self)
-    else:
-        s5 = dict(zip(SLOTS, outs[:8]))
-        s5_low, s5_high, s5_self = outs[8:]
-        clear(i >= 0, *outs[:8], s5_self)
-        clear(i < half_rows, s5_low)
-        clear(i >= half_rows, s5_high)
-
-    def put(values, fine_c_here):
-        rows = slice(0, values.shape[0])
-        high, low = split_parts(values)
+    s5 = dict(zip(SLOTS, outs[:8]))
+    s5_low, s5_high, s5_self = outs[8:11]
+    e6 = dict(zip(SLOTS, outs[11:19]))
+    d6 = dict(zip(SLOTS, outs[19:27]))
+    e6_rest, d6_self = outs[27:]
+    clear(i >= 0, *outs[:8], s5_self)
+    clear(i < half_rows, s5_low)
+    clear(i >= half_rows, s5_high)
+    clear(even, *outs[11:19], e6_rest)
+    clear(odd, *outs[19:27], d6_self)
+
+    def put(row_count, fine_c_here):
+        rows = slice(0, row_count)
         span = CG * N4 if fine_c_here else CG // 2 * N4
         reach = span + 2 * N4 if fine_c_here else span
         for k in range(GROUPS):
-            for place, piece in ((0, high), (reach, low)):
-                xb[k, rows, place : place + span] = piece[:, k * span : k * span + span]
-                if fine_c_here:
-                    ahead = (k + 1) % GROUPS * span
-                    xb[k, rows, place + span : place + reach] = piece[:, ahead : ahead + 2 * N4]
+            for lane in range(0, span, 2 * N4):
+                value = x_ref[0, 0, rows, k * span + lane : k * span + lane + 2 * N4]
+                for place, piece in zip((0, reach), split_parts(value)):
+                    xb[k, rows, place + lane : place + lane + 2 * N4] = piece
+                    if fine_c_here and lane == 0:
+                        before = (k + GROUPS - 1) % GROUPS
+                        xb[before, rows, place + span : place + reach] = piece
 
     for oc, od in CASES:
         for ob in range(2):
             @pl.when(active & (fine_b == ob) & (fine_c == oc) & (fine_d == od))
             def _(oc=oc, od=od, ob=ob):
-                lanes = N3 * N4 if oc else HC * N4
                 rows = (1 + ob) * HB
-                put(x_ref[0, 0, :rows, :lanes], oc)
+                put(rows, oc)
                 reach = (CG + 2) * N4 if oc else CG // 2 * N4
                 table = tables[oc, od][...]
                 lhs = xb[:, :rows, : 2 * reach].reshape(GROUPS * rows, 2 * reach)
@@ -228,33 +226,31 @@
     def line_of(ref):
         return lambda block, h, sx, sy: (ref, (h, sx, sy, 0))
 
-    if fine:
-        add_up(active & even, range(SHARED_D), slot_of(e6))
-        add_up(active & even, range(SHARED_D, SHARED_C), rest_of(e6_rest))
-        add_up(active & odd, range(SHARED_D), slot_of(d6))
-        add_up(active & odd, range(SHARED_D, SHARED_C), rest_of(d6_self))
-
-        @pl.when((g == count - 1) & (i > 0))
-        def _():
-            for slot in SLOTS:
-                d6[slot][...] -= 0.5 * e6[slot][...]
-            d6_self[...] -= 0.5 * e6_rest[...]
-    else:
-        five = active
-        add_up(five, range(SHARED_D), slot_of(s5))
-        add_up(five & (i < half_rows), range(SHARED_D, SHARED_C), rest_of(s5_low))
-        add_up(five & (i >= half_rows), range(SHARED_D, SHARED_C), rest_of(s5_high))
-        add_up(five, range(SHARED_C, 8), line_of(s5_self))
-
-
-def forward(fine, grids, scal, weight):
+    six = active & (level == 2)
+    five = active & (level == 1)
+    add_up(six & even, range(SHARED_D), slot_of(e6))
+    add_up(six & even, range(SHARED_D, SHARED_C), rest_of(e6_rest))
+    add_up(six & odd, range(SHARED_D), slot_of(d6))
+    add_up(six & odd, range(SHARED_D, SHARED_C), rest_of(d6_self))
+    add_up(five, range(SHARED_D), slot_of(s5))
+    add_up(five & (i < half_rows), range(SHARED_D, SHARED_C), rest_of(s5_low))
+    add_up(five & (i >= half_rows), range(SHARED_D, SHARED_C), rest_of(s5_high))
+    add_up(five, range(SHARED_C, 8), line_of(s5_self))
+
+    @pl.when((g == count - 1) & (i > 0))
+    def _():
+        for slot in SLOTS:
+            d6[slot][...] -= 0.5 * e6[slot][...]
+        d6_self[...] -= 0.5 * e6_rest[...]
+
+
+def forward(grids, scal, weight, after):
     count, rows_here = grids.shape[:2]
     half_rows = rows_here // 2
     tables = forward_tables()
     levels = scal[: 4 * count].reshape(count, 4)[:, 0]
     rows = scal[4 * count + 2] + jnp.arange(rows_here, dtype=jnp.int32)
-    takes = levels == (2 if fine else 1)
-    takes = takes[None, :] & (rows[:, None] < (N1 // 4) * (1 << levels)[None, :])
+    takes = (levels > 0)[None, :] & (rows[:, None] < (N1 // 4) * (1 << levels)[None, :])
     steps = jnp.arange(rows_here * count, dtype=jnp.int32)
     earlier = (steps[None, :] <= steps[:, None]) & takes.reshape(-1)[None, :]
     fetch = jnp.max(jnp.where(earlier, steps[None, :], 0), axis=1)
@@ -281,32 +277,33 @@
         return jnp.maximum(i - 1, 0) // 2
 
     rest = SHARED_C - SHARED_D
-    if fine:
-        out_specs = (
-            [rows_spec(SHARED_D, even_row)] * 8
-            + [rows_spec(SHARED_D, odd_row)] * 8
-            + [rest_spec(rest, even_row), rest_spec(rest, odd_row)]
-        )
-        out_shape = [shape(SHARED_D, half_rows)] * 16 + [shape(2, 2, 2, rest, half_rows)] * 2
-    else:
-        out_specs = [rows_spec(SHARED_D, lambda i: i)] * 8 + [
+    out_specs = (
+        [rows_spec(SHARED_D, lambda i: i)] * 8
+        + [
             rest_spec(rest, lambda i: jnp.minimum(i, half_rows - 1)),
             rest_spec(rest, lambda i: jnp.maximum(i - half_rows, 0)),
             line_spec(lambda i: i),
         ]
-        out_shape = (
-            [shape(SHARED_D, rows_here)] * 8
-            + [shape(2, 2, 2, rest, half_rows)] * 2
-            + [shape(2, 2, 2, rows_here)]
-        )
+        + [rows_spec(SHARED_D, even_row)] * 8
+        + [rows_spec(SHARED_D, odd_row)] * 8
+        + [rest_spec(rest, even_row), rest_spec(rest, odd_row)]
+    )
+    out_shape = (
+        [shape(SHARED_D, rows_here)] * 8
+        + [shape(2, 2, 2, rest, half_rows)] * 2
+        + [shape(2, 2, 2, rows_here)]
+        + [shape(SHARED_D, half_rows)] * 16
+        + [shape(2, 2, 2, rest, half_rows)] * 2
+    )
     ordered = [tables[case] for case in CASES]
     return pl.pallas_call(
-        lambda *refs: forward_kernel(fine, rows_here, count, *refs),
+        lambda *refs: forward_kernel(rows_here, count, *refs),
         grid_spec=pltpu.PrefetchScalarGridSpec(
             num_scalar_prefetch=3,
             grid=(rows_here, count),
             in_specs=[pl.BlockSpec((1, 1, N2, N3 * N4), page)]
-            + [constant(table) for table in ordered],
+            + [constant(table) for table in ordered]
+            + [pl.BlockSpec(memory_space=pl.ANY)],
             out_specs=out_specs,
             scratch_shapes=[
                 pltpu.VMEM((GROUPS, 2 * HB, 2 * (CG + 2) * N4), jnp.bfloat16),
@@ -318,18 +315,18 @@
         cost_estimate=pl.CostEstimate(
             flops=10**10, bytes_accessed=60 * 2**20, transcendentals=0
         ),
-        name="split_fine" if fine else "split_coarse",
-    )(scal, fetch, weight, grids, *ordered)
+        name="split_grids",
+    )(scal, fetch, weight, grids, *ordered, after)
 
 
 def coarsest_kernel(count, scal, weight, x_ref, table, out, yb):
     i = pl.program_id(0)
-    g = pl.program_id(1)
     mine_x = scal[4 * count]
     mine_y = scal[4 * count + 1]
+    g = scal[4 * count + 3]
     active = (scal[4 * g] == 0) & (scal[4 * count + 2] + i < N1 // 4)
 
-    @pl.when(g == 0)
+    @pl.when(jnp.logical_not(active))
     def _():
         out[...] = jnp.zeros_like(out)
 
@@ -346,7 +343,7 @@
             quarter = 2 * (sx ^ mine_x) + (sy ^ mine_y)
             start = pl.multiple_of(quarter * QR, QR)
             for j in range(GROUPS // 2):
-                out[h, sx, sy, 0, :, j * TILE : j * TILE + TILE] += yb[
+                out[h, sx, sy, 0, :, j * TILE : j * TILE + TILE] = yb[
                     h * (GROUPS // 2) + j, pl.ds(start, QR)
                 ]
 
@@ -355,18 +352,19 @@
     count, rows_here = grids.shape[:2]
     table = forward_tables()[0, 0]
 
-    def page(i, g, scal, weight):
+    def page(i, scal, weight):
+        g = scal[4 * count + 3]
         wanted = (scal[4 * g] == 0) & (scal[4 * count + 2] + i < N1 // 4)
-        return (jnp.where(wanted, g, 0), jnp.where(wanted, i, 0), 0, 0)
+        return (g, jnp.where(wanted, i, 0), 0, 0)
 
     return pl.pallas_call(
         lambda *refs: coarsest_kernel(count, *refs),
         grid_spec=pltpu.PrefetchScalarGridSpec(
             num_scalar_prefetch=2,
-            grid=(rows_here, count),
+            grid=(rows_here,),
             in_specs=[
                 pl.BlockSpec((1, 1, HB, HC * N4), page),
-                pl.BlockSpec(table.shape, lambda i, g, *_: (0, 0)),
+                pl.BlockSpec(table.shape, lambda i, *_: (0, 0)),
             ],
             out_specs=line_spec(lambda i: i),
             scratch_shapes=[pltpu.VMEM((GROUPS, HB, TILE), jnp.float32)],
@@ -388,33 +386,28 @@
 
 def line_spec(row_of):
     return pl.BlockSpec(
-        (2, 2, 2, 1, QR, HALF_LANES), lambda i, g, *_: (0, 0, 0, row_of(i), 0, 0)
-    )
-
-
-def backward_kernel(fine, rows_here, count, scal, order, *refs):
-    used = 7 if fine else 20
+        (2, 2, 2, 1, QR, HALF_LANES), lambda i, *_: (0, 0, 0, row_of(i), 0, 0)
+    )
+
+
+def backward_kernel(rows_here, count, scal, *refs):
+    used = 19
     c6, c6_next, c6_rest, c6_rest_next, ahead_row, d6, d6_self = refs[:7]
-    if not fine:
-        c5 = dict(zip(SLOTS, refs[7:15]))
-        c5_low, c5_high, s5_self = refs[15:18]
-        c4 = refs[18]
+    c5 = dict(zip(SLOTS, refs[7:15]))
+    c5_low, c5_high, s5_self, c4 = refs[15:19]
     tables = dict(zip(CASES, refs[used : used + 4]))
     out = refs[used + 4]
     coarse, detail, joined, xb = refs[used + 5 :]
     half_rows = rows_here // 2
     i = pl.program_id(0)
-    slot_number = pl.program_id(1)
-    g = order[slot_number]
+    g = pl.program_id(1)
     level, fine_b, fine_c, fine_d = grid_facts(scal, g)
     mine_x = scal[4 * count]
     mine_y = scal[4 * count + 1]
     row = scal[4 * count + 2] + i
     odd = lax.rem(i, 2) == 1
     even = lax.rem(i, 2) == 0
-    fresh = slot_number < order[count]
-    inside = row < (N1 // 4) * (1 << level)
-    active = fresh & inside
+    active = row < (N1 // 4) * (1 << level)
 
     def stage(wanted, blocks, source):
         for block in blocks:
@@ -454,16 +447,15 @@
     if half_rows > 1:
         stage((level == 2) & odd & (i < rows_here - 1), range(SHARED_C), between(False))
     stage((level == 2) & odd & (i == rows_here - 1), range(SHARED_C), between(True))
-    if not fine:
-        rest = range(SHARED_D, SHARED_C)
-        five = level == 1
-        stage(five, range(SHARED_D), lambda b, h, x, y: c5[h, x, y][b, 0])
-        stage(five & (i < half_rows), rest, lambda b, h, x, y: c5_low[h, x, y, b - SHARED_D, 0])
-        stage(five & (i >= half_rows), rest, lambda b, h, x, y: c5_high[h, x, y, b - SHARED_D, 0])
-        stage(five, range(SHARED_C, 8), lambda b, h, x, y: s5_self[h, x, y, 0])
-        stage(level == 0, range(1), lambda b, h, x, y: c4[h, x, y, 0])
-
-    @pl.when(fresh & jnp.logical_not(inside))
+    rest = range(SHARED_D, SHARED_C)
+    five = level == 1
+    stage(five, range(SHARED_D), lambda b, h, x, y: c5[h, x, y][b, 0])
+    stage(five & (i < half_rows), rest, lambda b, h, x, y: c5_low[h, x, y, b - SHARED_D, 0])
+    stage(five & (i >= half_rows), rest, lambda b, h, x, y: c5_high[h, x, y, b - SHARED_D, 0])
+    stage(five, range(SHARED_C, 8), lambda b, h, x, y: s5_self[h, x, y, 0])
+    stage(level == 0, range(1), lambda b, h, x, y: c4[h, x, y, 0])
+
+    @pl.when(jnp.logical_not(active))
     def _():
         out[...] = jnp.zeros_like(out)
 
@@ -508,30 +500,13 @@
                     out[0, 0, :, HC * N4 :] = jnp.zeros((N2, HC * N4), jnp.float32)
 
 
-def backward(fine, count, scal, rows_here, values, before=None):
+def backward(count, scal, rows_here, values):
     half_rows = rows_here // 2
     tables = backward_tables()
     ordered = [tables[case] for case in CASES]
-    levels = scal[: 4 * count].reshape(count, 4)[:, 0]
-    takes = (levels == 2) if fine else (levels < 2)
-    number = jnp.maximum(jnp.sum(takes.astype(jnp.int32)), 1)
-    spots = jnp.arange(count, dtype=jnp.int32)
-    before_me = (spots[None, :] < spots[:, None]).astype(jnp.int32)
-    takes_int = takes.astype(jnp.int32)
-    rank = jnp.where(
-        takes,
-        jnp.sum(before_me * takes_int[None, :], axis=1),
-        jnp.sum(takes_int) + jnp.sum(before_me * (1 - takes_int)[None, :], axis=1),
-    )
-    wanted = jnp.minimum(spots, number - 1)
-    order = jnp.sum(jnp.where(rank[None, :] == wanted[:, None], spots[None, :], 0), axis=1)
-    order = jnp.concatenate([order, number[None]]).astype(jnp.int32)
 
     def constant(table):
         return pl.BlockSpec(table.shape, lambda i, g, *_: (0, 0))
-
-    def page(i, g, scal, order):
-        return (order[g], i, 0, 0)
 
     rest = SHARED_C - SHARED_D
     c6, c6_rest, ahead_row, d6, d6_self = values[:5]
@@ -546,28 +521,25 @@
         rest_spec(SHARED_D, lambda i: i // 2),
         rest_spec(rest, lambda i: i // 2),
     ]
-    aliases = {}
-    if not fine:
-        c5, c5_low, c5_high, s5_self = values[5:]
-        operands += [c5[slot] for slot in SLOTS] + [c5_low, c5_high, s5_self]
-        in_specs += [
-            pl.BlockSpec((SHARED_D, 1, QR, HALF_LANES), lambda i, g, *_: (0, i, 0, 0))
-        ] * 8 + [
-            rest_spec(rest, lambda i: jnp.minimum(i, half_rows - 1)),
-            rest_spec(rest, lambda i: jnp.maximum(i - half_rows, 0)),
-            line_spec(lambda i: i),
-        ]
-        c4 = jnp.stack([c5[slot][SHARED_D] for slot in SLOTS])
-        operands += [c4.reshape((2, 2, 2) + c4.shape[1:]), before]
-        in_specs += [line_spec(lambda i: i), pl.BlockSpec(memory_space=pl.ANY)]
-        aliases = {2 + len(operands) - 1: 0}
+    c5, c5_low, c5_high, s5_self = values[5:]
+    operands += [c5[slot] for slot in SLOTS] + [c5_low, c5_high, s5_self]
+    in_specs += [
+        pl.BlockSpec((SHARED_D, 1, QR, HALF_LANES), lambda i, g, *_: (0, i, 0, 0))
+    ] * 8 + [
+        rest_spec(rest, lambda i: jnp.minimum(i, half_rows - 1)),
+        rest_spec(rest, lambda i: jnp.maximum(i - half_rows, 0)),
+        line_spec(lambda i: i),
+    ]
+    c4 = jnp.stack([c5[slot][SHARED_D] for slot in SLOTS])
+    operands.append(c4.reshape((2, 2, 2) + c4.shape[1:]))
+    in_specs.append(line_spec(lambda i: i))
     return pl.pallas_call(
-        lambda *refs: backward_kernel(fine, rows_here, count, *refs),
+        lambda *refs: backward_kernel(rows_here, count, *refs),
         grid_spec=pltpu.PrefetchScalarGridSpec(
-            num_scalar_prefetch=2,
+            num_scalar_prefetch=1,
             grid=(rows_here, count),
             in_specs=in_specs + [constant(table) for table in ordered],
-            out_specs=pl.BlockSpec((1, 1, N2, N3 * N4), page),
+            out_specs=pl.BlockSpec((1, 1, N2, N3 * N4), lambda i, g, *_: (g, i, 0, 0)),
             scratch_shapes=[
                 pltpu.VMEM((4, GROUPS, HB + QR, TILE), jnp.float32),
                 pltpu.VMEM((4, GROUPS, HB, TILE), jnp.float32),
@@ -576,13 +548,12 @@
             ],
         ),
         out_shape=jax.ShapeDtypeStruct((count, rows_here, N2, N3 * N4), jnp.float32),
-        input_output_aliases=aliases,
         compiler_params=pltpu.CompilerParams(vmem_limit_bytes=60 * 2**20),
         cost_estimate=pl.CostEstimate(
             flops=10**10, bytes_accessed=60 * 2**20, transcendentals=0
         ),
-        name="join_fine" if fine else "join_coarse",
-    )(scal, order, *operands, *ordered)
+        name="join_grids",
+    )(scal, *operands, *ordered)
 
 
 def stack_slots(pieces):
@@ -677,7 +648,8 @@
             lax.axis_index("dom") * rows_here,
         ]
     ).astype(jnp.int32)
-    scal = jnp.concatenate([own_offsets.reshape(-1), place])
+    first = jnp.argmax(own_offsets[:, 0] == 0).astype(jnp.int32)
+    scal = jnp.concatenate([own_offsets.reshape(-1), place, first[None]])
     sources = dom_size // 2
     quarter_devices = dom_size // 4
     s4 = coarsest(grids, scal, own_weights)[:, :, :, None]
@@ -690,13 +662,12 @@
     spread = rows_up(spread, quarter_devices)
     coarsest_rows = rows_up(spread, sources)
 
-    coarse_parts = forward(False, grids, scal, own_weights)
-    s5 = dict(zip(SLOTS, coarse_parts[:8]))
-    s5_low, s5_high, s5_self = coarse_parts[8:]
-    fine_parts = forward(True, grids, scal, own_weights)
-    e6 = dict(zip(SLOTS, fine_parts[:8]))
-    d6 = dict(zip(SLOTS, fine_parts[8:16]))
-    e6_rest, d6_self = fine_parts[16:]
+    parts = forward(grids, scal, own_weights, s4)
+    s5 = dict(zip(SLOTS, parts[:8]))
+    s5_low, s5_high, s5_self = parts[8:11]
+    e6 = dict(zip(SLOTS, parts[11:19]))
+    d6 = dict(zip(SLOTS, parts[19:27]))
+    e6_rest, d6_self = parts[27:]
 
     from_low = lax.ppermute(s5_low, "dom", [(d, 2 * d) for d in range(sources)])
     from_high = lax.ppermute(s5_high, "dom", [(d, 2 * d + 1) for d in range(sources)])
@@ -754,9 +725,8 @@
     c5_low = lax.ppermute(c6_rest, "dom", [(2 * d, d) for d in range(sources)])
     c5_high = lax.ppermute(c6_rest, "dom", [(2 * d + 1, d) for d in range(sources)])
     values = [c6, c6_rest, ahead_row, d6, d6_self]
-    written = backward(True, count, scal, rows_here, values)
     values += [c5, c5_low, c5_high, s5_self]
-    return backward(False, count, scal, rows_here, values, written)
+    return backward(count, scal, rows_here, values)
 
 
 def solution(mesh):

time: 481 us -> 457 us (0.950)
  waiting for transfers between devices: 157 us -> 205 us
  Pallas kernels: 154 us -> 108 us
  starting transfers between devices: 123 us -> 113 us
  other arithmetic: 23.1 us -> 15.6 us
  local copies, waits for them, and re-layouts: 18.2 us -> 11.4 us
    ppermute x54, waiting for transfers between devices: 104 us -> 149 us  [exchange(): return lax.ppermute(value, ('half', 'grid', 'dom'), pairs)]
    pallas_call x4 -> x2, Pallas kernels: 137 us -> 101 us  [the longest x1 52.9 us: backward(): pl.pallas_call(lambda *refs: backward_kernel(rows_here, count, *refs), gr...]
    pallas_call x1, Pallas kernels: 17 us -> 7.2 us  [coarsest(): pl.pallas_call(lambda *refs: coarsest_kernel(count, *refs), grid_spec=plt...]
    ppermute x3, starting transfers between devices: 14.2 us -> 6.25 us  [rows_up(): lax.ppermute(value[..., half_rows:, :, :], 'dom', [(d, 2 * d + 1) for d i...]
  transfers between devices with their start and end apart: 73 -> 73, of which waited for: 29 -> 33; matrix products, arithmetic and copies ran while one was open for 7% -> 3% of each run, Pallas kernels for 20% -> 0%
where the time goes in v1:
time: 457 us; the launch traced here: 455 us
  waiting for transfers between devices  205 us (45%)
  starting transfers between devices  113 us (25%)
  Pallas kernels  108 us (24%)
  other arithmetic  15.6 us (3%)
  local copies, waits for them, and re-layouts  11.4 us (2%)
    ppermute x54, waiting for transfers between devices, exchange(): return lax.ppermute(value, ('half', 'grid', 'dom'), pairs)  149 us
    ppermute x54, starting transfers between devices, exchange(): return lax.ppermute(value, ('half', 'grid', 'dom'), pairs)  85.8 us
    ppermute x4, waiting for transfers between devices, per_device(): lax.ppermute(c6_own[..., :1, ::2, :, :], 'dom', [(4 * d + r, d) for d in...  54.4 us
    pallas_call x1, Pallas kernels, backward(): pl.pallas_call(lambda *refs: backward_kernel(rows_here, count, *refs), gr...  52.9 us
    pallas_call x1, Pallas kernels, forward(): pl.pallas_call(lambda *refs: forward_kernel(rows_here, count, *refs), gri...  48.2 us
  transfers between devices with their start and end apart: 73, of which 33 were waited for; matrix products, arithmetic and copies ran while one was open for 3% of the time, Pallas kernels for 0%

profile of v1, /device:TPU:0, one launch (start us, length us, event | category | flops | bytes accessed | tf_op | source)
XLA Modules:
  0.0 454.7 jit_solution(9927849777995892109)
XLA Ops:
  8.0 7.2 %split_coarsest.1 = f32[2,2,2,8,8,512]{5,4,3,2,1,0:T(8,128)} custom-call(s32[20]{0:T(128)} %concatenate.55.refs_0_, f32[4]{0:T(128)} %dynamic_slice.7.refs_1_.refs_2_, f32[4,8,64,4096]{3,2,1,0:T(8,128)} %refs_3_.2, bf16[256,128]{1,0:T(8,128)(2,1)} %constant.428.clone.refs_3_.refs_4_), custom_call_target="tpu_custom_call" | custom-call | flops 100000000 | bytes 4194304 | tf_op jit(solution)/shard_map/split_coarsest/pallas_call | solution.py:360
  15.2 48.2 %split_grids.1 = (f32[4,8,8,512]{3,2,1,0:T(8,128)}, f32[4,8,8,512]{3,2,1,0:T(8,128)}, f32[4,8,8,512]{3,2,1,0:T(8,128)}, f32[4,8,8,512]{3,2,1,0:T(8,128)}, f32[4,...) custom-call(s32[20]{0:T(128)} %concatenate.55.refs_0_, ...), custom_call_target="tpu_custom_call" | custom-call | flops 10000000000 | bytes 62914560 | tf_op jit(solution)/shard_map/split_grids/pallas_call | solution.py:299
  72.0 3.9 collective-permute-start.12
  80.3 16.7 %collective-permute-done.12 = f32[4,8,8,512]{3,2,1,0:T(8,128)S(1)} collective-permute-done((f32[4,8,8,512]{3,2,1,0:T(8,128)S(1)}, f32[4,8,8,512]{3,2,1,0:T(8,128)S(1)}, u32[]{:S(2)}, u32[]{:S(2)}) %collective-permute-start.12) | collective-permute-done | bytes 524320 | tf_op jit(solution)/shard_map/ppermute | solution.py:578
  99.8 4.1 collective-permute-start.13
  109.7 4.8 %collective-permute-done.14 = f32[4,8,8,512]{3,2,1,0:T(8,128)S(1)} collective-permute-done((f32[4,8,8,512]{3,2,1,0:T(8,128)S(1)}, f32[4,8,8,512]{3,2,1,0:T(8,128)S(1)}, u32[]{:S(2)}, u32[]{:S(2)}) %collective-permute-start.14) | collective-permute-done | bytes 524320 | tf_op jit(solution)/shard_map/ppermute | solution.py:578
  115.2 9.3 %collective-permute-done.13 = f32[4,8,8,512]{3,2,1,0:T(8,128)S(1)} collective-permute-done((f32[4,8,8,512]{3,2,1,0:T(8,128)S(1)}, f32[4,8,8,512]{3,2,1,0:T(8,128)S(1)}, u32[]{:S(2)}, u32[]{:S(2)}) %collective-permute-start.13) | collective-permute-done | bytes 524320 | tf_op jit(solution)/shard_map/ppermute | solution.py:578
  129.2 6.1 %collective-permute-done.54 = f32[4,4,8,512]{3,2,1,0:T(8,128)S(1)} collective-permute-done((f32[4,4,8,512]{3,2,1,0:T(8,128)S(1)}, f32[4,4,8,512]{3,2,1,0:T(8,128)S(1)}, u32[]{:S(2)}, u32[]{:S(2)}) %collective-permute-start.54) | collective-permute-done | bytes 262176 | tf_op jit(solution)/shard_map/ppermute | solution.py:578
  140.1 6.4 %collective-permute-done.55 = f32[4,4,8,512]{3,2,1,0:T(8,128)S(1)} collective-permute-done((f32[4,4,8,512]{3,2,1,0:T(8,128)S(1)}, f32[4,4,8,512]{3,2,1,0:T(8,128)S(1)}, u32[]{:S(2)}, u32[]{:S(2)}) %collective-permute-start.55) | collective-permute-done | bytes 262176 | tf_op jit(solution)/shard_map/ppermute | solution.py:578
  162.7 3.5 collective-permute-done.28
  173.7 3.1 collective-permute-start.29
  179.6 6.7 %collective-permute-done.29 = f32[3,4,8,512]{3,2,1,0:T(8,128)S(1)} collective-permute-done((f32[3,4,8,512]{3,2,1,0:T(8,128)S(1)}, f32[3,4,8,512]{3,2,1,0:T(8,128)S(1)}, u32[]{:S(2)}, u32[]{:S(2)}) %collective-permute-start.29) | collective-permute-done | bytes 196640 | tf_op jit(solution)/shard_map/ppermute | solution.py:578
  190.3 3.4 collective-permute-start.18
  197.5 3.2 collective-permute-done.30
  211.9 45.3 %collective-permute-done.62 = f32[2,1,2,8,512]{4,3,2,1,0:T(8,128)S(1)} collective-permute-done((f32[2,1,2,8,512]{4,3,2,1,0:T(8,128)S(1)}, f32[2,1,2,8,512]{4,3,2,1,0:T(8,128)S(1)}, u32[]{:S(2)}, u32[]{:S(2)}) %collective-permute-start.62) | collective-permute-done | bytes 65568 | tf_op jit(solution)/shard_map/ppermute | solution.py:699
  258.5 4.8 %collective-permute-done.63 = f32[2,1,2,8,512]{4,3,2,1,0:T(8,128)S(1)} collective-permute-done((f32[2,1,2,8,512]{4,3,2,1,0:T(8,128)S(1)}, f32[2,1,2,8,512]{4,3,2,1,0:T(8,128)S(1)}, u32[]{:S(2)}, u32[]{:S(2)}) %collective-permute-start.63) | collective-permute-done | bytes 65568 | tf_op jit(solution)/shard_map/ppermute | solution.py:699
  264.6 4.3 collective-permute-done.64
  270.2 5.4 %collective-permute-start.39 = (f32[2,7,1,8,512]{4,3,2,1,0:T(8,128)S(1)}, f32[2,7,1,8,512]{4,3,2,1,0:T(8,128)S(1)}, u32[]{:S(2)}, u32[]{:S(2)}) collective-permute-start(f32[2,7,1,8,512]{4,3,2,1,0:T(8,128)S(1)} %fusion.6), channel_id=1, source_target_pairs={{1,0},{2,1},{3,2},{4,3},{5,4},{6,5},{7,6},{0,7},{9,8},{10,9},{11,1... | collective-permute-start | bytes 688136 | tf_op jit(solution)/shard_map/ppermute | solution.py:623
  295.4 3.5 collective-permute-done.40
  300.4 4.1 collective-permute-done.43
  306.6 3.9 collective-permute-done.42
  312.6 6.0 %collective-permute-done.44 = f32[7,1,8,512]{3,2,0,1:T(8,128)S(1)} collective-permute-done((f32[7,1,8,512]{3,2,0,1:T(8,128)S(1)}, f32[7,1,8,512]{3,2,0,1:T(8,128)S(1)}, u32[]{:S(2)}, u32[]{:S(2)}) %collective-permute-start.44) | collective-permute-done | bytes 114720 | tf_op jit(solution)/shard_map/ppermute | solution.py:578
  320.9 3.4 collective-permute-start.65
  324.3 5.9 %collective-permute-done.45 = f32[7,1,8,512]{3,2,0,1:T(8,128)S(1)} collective-permute-done((f32[7,1,8,512]{3,2,0,1:T(8,128)S(1)}, f32[7,1,8,512]{3,2,0,1:T(8,128)S(1)}, u32[]{:S(2)}, u32[]{:S(2)}) %collective-permute-start.45) | collective-permute-done | bytes 114720 | tf_op jit(solution)/shard_map/ppermute | solution.py:578
  333.4 3.1 collective-permute-start.66
  340.7 3.1 collective-permute-start.67
  345.6 20.6 %collective-permute-done.69.refs_14_ = f32[5,8,8,512]{3,2,1,0:T(8,128)S(1)} collective-permute-done((f32[5,8,8,512]{3,2,1,0:T(8,128)S(1)}, f32[5,8,8,512]{3,2,1,0:T(8,128)S(1)}, u32[]{:S(2)}, u32[]{:S(2)}) %collective-permute-start.69) | collective-permute-done | bytes 655392 | tf_op jit(solution)/shard_map/ppermute | solution.py:578
  366.3 3.4 collective-permute-start.68
  372.4 7.9 %collective-permute-done.67.refs_11_ = f32[5,8,8,512]{3,2,1,0:T(8,128)S(1)} collective-permute-done((f32[5,8,8,512]{3,2,1,0:T(8,128)S(1)}, f32[5,8,8,512]{3,2,1,0:T(8,128)S(1)}, u32[]{:S(2)}, u32[]{:S(2)}) %collective-permute-start.67) | collective-permute-done | bytes 655392 | tf_op jit(solution)/shard_map/ppermute | solution.py:578
  380.3 4.9 %collective-permute-done.68.refs_13_ = f32[5,8,8,512]{3,2,1,0:T(8,128)S(1)} collective-permute-done((f32[5,8,8,512]{3,2,1,0:T(8,128)S(1)}, f32[5,8,8,512]{3,2,1,0:T(8,128)S(1)}, u32[]{:S(2)}, u32[]{:S(2)}) %collective-permute-start.68) | collective-permute-done | bytes 655392 | tf_op jit(solution)/shard_map/ppermute | solution.py:578
  385.3 14.0 %collective-permute-done.70.refs_15_ = f32[5,8,8,512]{3,2,1,0:T(8,128)S(1)} collective-permute-done((f32[5,8,8,512]{3,2,1,0:T(8,128)S(1)}, f32[5,8,8,512]{3,2,1,0:T(8,128)S(1)}, u32[]{:S(2)}, u32[]{:S(2)}) %collective-permute-start.70) | collective-permute-done | bytes 655392 | tf_op jit(solution)/shard_map/ppermute | solution.py:578
  401.7 52.9 %join_grids.1 = f32[4,8,64,4096]{3,2,1,0:T(8,128)} custom-call(s32[20]{0:T(128)} %concatenate.55.refs_0_, f32[2,2,2,4,4,8,512]{6,5,4,3,2,1,0:T(8,128)} %pad_maximum_fusion.1.refs_1_.refs_2_, f32[2,2,2,4,4,8,512]{6,5,4,3,2,1,0:T(8,128)} %pad_maximum_fusion.1.refs_1_.refs_2_, f32[2,2,2,3,4,8,512]{6,5,4,3,2,1,0:T(8,128)} %copy-done, ...), custom_call_target="tpu_custom_call" | custom-call | flops 10000000000 | bytes 62914560 | tf_op jit(solution)/shard_map/join_grids/pallas_call | solution.py:536
  (314 shorter events, 130.3 us)
Async XLA Ops:
  66.6 33.2 %collective-permute-start.46 = (f32[2,2,2,7,1,8,512]{6,5,4,3,2,1,0:T(8,128)S(1)}, f32[2,2,2,7,1,8,512]{6,5,4,3,2,1,0:T(8,128)S(1)}, u32[]{:S(2)}, u32[]{:S(2)}) collective-permute-start(f32[2,2,2,7,1,8,512]{6,5,4,3,2,1,0:T(8,128)S(1)} %pad_maximum_fusion.6), channel_id=1, source_target_pairs={{1,0},{2,1},{3,2},{4,3},{5,4},{6,5},{7,6},{0,7},{9,8},{10,9},{11,1... | collective-permute-start | bytes 2752520 | tf_op jit(solution)/shard_map/ppermute | solution.py:623
  70.0 37.2 %collective-permute-start.11 = (f32[4,8,8,512]{3,2,1,0:T(8,128)S(1)}, f32[4,8,8,512]{3,2,1,0:T(8,128)S(1)}, u32[]{:S(2)}, u32[]{:S(2)}) collective-permute-start(f32[4,8,8,512]{3,2,1,0:T(8,128)S(1)} %copy-done.37), channel_id=1, source_target_pairs={{0,16},{1,17},{2,18},{3,19},{8,24},{9,25},{10,26},{11,27},{16,0},{... | collective-permute-start | bytes 1572872 | tf_op jit(solution)/shard_map/ppermute | solution.py:578
  72.0 25.0 %collective-permute-start.12 = (f32[4,8,8,512]{3,2,1,0:T(8,128)S(1)}, f32[4,8,8,512]{3,2,1,0:T(8,128)S(1)}, u32[]{:S(2)}, u32[]{:S(2)}) collective-permute-start(f32[4,8,8,512]{3,2,1,0:T(8,128)S(1)} %copy-done.39), channel_id=1, source_target_pairs={{0,16},{1,17},{2,18},{3,19},{8,24},{9,25},{10,26},{11,27},{16,0},{... | collective-permute-start | bytes 1572872 | tf_op jit(solution)/shard_map/ppermute | solution.py:578
  75.9 21.8 %collective-permute-start.15 = (f32[4,8,8,512]{3,2,1,0:T(8,128)S(1)}, f32[4,8,8,512]{3,2,1,0:T(8,128)S(1)}, u32[]{:S(2)}, u32[]{:S(2)}) collective-permute-start(f32[4,8,8,512]{3,2,1,0:T(8,128)S(1)} %copy-done.38), channel_id=1, source_target_pairs={{0,8},{1,9},{2,10},{3,11},{8,0},{9,1},{10,2},{11,3},{16,24},{17,25... | collective-permute-start | bytes 1572872 | tf_op jit(solution)/shard_map/ppermute | solution.py:578
  78.8 47.7 %collective-permute-start.2 = (f32[2,2,2,1,8,8,512]{6,5,4,3,2,1,0:T(8,128)S(1)}, f32[2,2,2,1,8,8,512]{6,5,4,3,2,1,0:T(8,128)S(1)}, u32[]{:S(2)}, u32[]{:S(2)}) collective-permute-start(f32[2,2,2,1,8,8,512]{6,5,4,3,2,1,0:T(8,128)S(1)} %get-tuple-element.269), channel_id=1, source_target_pairs={{0,1},{1,3},{8,9},{9,11},{16,17},{17,19},{24,25},{25,27}} | collective-permute-start | bytes 3145736 | tf_op jit(solution)/shard_map/ppermute | solution.py:609
  97.0 31.2 %collective-permute-start.1 = (f32[2,2,2,1,8,8,512]{6,5,4,3,2,1,0:T(8,128)S(1)}, f32[2,2,2,1,8,8,512]{6,5,4,3,2,1,0:T(8,128)S(1)}, u32[]{:S(2)}, u32[]{:S(2)}) collective-permute-start(f32[2,2,2,1,8,8,512]{6,5,4,3,2,1,0:T(8,128)S(1)} %get-tuple-element.270), channel_id=1, source_target_pairs={{0,0},{1,2},{8,8},{9,10},{16,16},{17,18},{24,24},{25,26}} | collective-permute-start | bytes 3145736 | tf_op jit(solution)/shard_map/ppermute | solution.py:608
  99.8 24.7 %collective-permute-start.13 = (f32[4,8,8,512]{3,2,1,0:T(8,128)S(1)}, f32[4,8,8,512]{3,2,1,0:T(8,128)S(1)}, u32[]{:S(2)}, u32[]{:S(2)}) collective-permute-start(f32[4,8,8,512]{3,2,1,0:T(8,128)S(1)} %add.271), channel_id=1, source_target_pairs={{0,8},{1,9},{2,10},{3,11},{8,0},{9,1},{10,2},{11,3},{16,24},{17,25... | collective-permute-start | bytes 1572872 | tf_op jit(solution)/shard_map/ppermute | solution.py:578
  114.5 35.4 %collective-permute-start.25 = (f32[2,2,2,3,4,8,512]{6,5,4,3,2,1,0:T(8,128)S(1)}, f32[2,2,2,3,4,8,512]{6,5,4,3,2,1,0:T(8,128)S(1)}, u32[]{:S(2)}, u32[]{:S(2)}) collective-permute-start(f32[2,2,2,3,4,8,512]{6,5,4,3,2,1,0:T(8,128)S(1)} %copy-done.35), channel_id=1, source_target_pairs={{0,0},{1,2},{2,4},{3,6},{8,8},{9,10},{10,12},{11,14},{16,16},{17,1... | collective-permute-start | bytes 4718600 | tf_op jit(solution)/shard_map/ppermute | solution.py:672
  124.5 26.2 %collective-permute-start.26 = (f32[2,2,2,3,4,8,512]{6,5,4,3,2,1,0:T(8,128)S(1)}, f32[2,2,2,3,4,8,512]{6,5,4,3,2,1,0:T(8,128)S(1)}, u32[]{:S(2)}, u32[]{:S(2)}) collective-permute-start(f32[2,2,2,3,4,8,512]{6,5,4,3,2,1,0:T(8,128)S(1)} %copy-done.34), channel_id=1, source_target_pairs={{0,1},{1,3},{2,5},{3,7},{8,9},{9,11},{10,13},{11,15},{16,17},{17,1... | collective-permute-start | bytes 4718600 | tf_op jit(solution)/shard_map/ppermute | solution.py:673
  150.7 21.2 %collective-permute-start.51 = (f32[4,4,8,512]{3,2,1,0:T(8,128)S(1)}, f32[4,4,8,512]{3,2,1,0:T(8,128)S(1)}, u32[]{:S(2)}, u32[]{:S(2)}) collective-permute-start(f32[4,4,8,512]{3,2,1,0:T(8,128)S(1)} %add_add_fusion.2), channel_id=1, source_target_pairs={{0,16},{1,17},{2,18},{3,19},{4,20},{5,21},{6,22},{7,23},{8,24},{9,... | collective-permute-start | bytes 786440 | tf_op jit(solution)/shard_map/ppermute | solution.py:578
  154.0 23.0 %collective-permute-start.27 = (f32[3,4,8,512]{3,2,1,0:T(8,128)S(1)}, f32[3,4,8,512]{3,2,1,0:T(8,128)S(1)}, u32[]{:S(2)}, u32[]{:S(2)}) collective-permute-start(f32[3,4,8,512]{3,2,1,0:T(8,128)S(1)} %get-tuple-element.273), channel_id=1, source_target_pairs={{0,16},{1,17},{2,18},{3,19},{4,20},{5,21},{6,22},{7,23},{8,24},{9,... | collective-permute-start | bytes 589832 | tf_op jit(solution)/shard_map/ppermute | solution.py:578
  157.7 19.3 %collective-permute-start.34 = (f32[3,4,8,512]{3,2,1,0:T(8,128)S(1)}, f32[3,4,8,512]{3,2,1,0:T(8,128)S(1)}, u32[]{:S(2)}, u32[]{:S(2)}) collective-permute-start(f32[3,4,8,512]{3,2,1,0:T(8,128)S(1)} %get-tuple-element.274), channel_id=1, source_target_pairs={{0,8},{1,9},{2,10},{3,11},{4,12},{5,13},{6,14},{7,15},{8,0},{9,1},... | collective-permute-start | bytes 589832 | tf_op jit(solution)/shard_map/ppermute | solution.py:578
  169.3 25.1 %collective-permute-start.33 = (f32[3,4,8,512]{3,2,1,0:T(8,128)S(1)}, f32[3,4,8,512]{3,2,1,0:T(8,128)S(1)}, u32[]{:S(2)}, u32[]{:S(2)}) collective-permute-start(f32[3,4,8,512]{3,2,1,0:T(8,128)S(1)} %get-tuple-element.275), channel_id=1, source_target_pairs={{0,8},{1,9},{2,10},{3,11},{4,12},{5,13},{6,14},{7,15},{8,0},{9,1},... | collective-permute-start | bytes 589832 | tf_op jit(solution)/shard_map/ppermute | solution.py:578
  176.9 19.7 %collective-permute-start.8 = (f32[4,4,8,512]{3,2,1,0:T(8,128)S(1)}, f32[4,4,8,512]{3,2,1,0:T(8,128)S(1)}, u32[]{:S(2)}, u32[]{:S(2)}) collective-permute-start(f32[4,4,8,512]{3,2,1,0:T(8,128)S(1)} %get-tuple-element.298), channel_id=1, source_target_pairs={{0,8},{1,9},{2,10},{3,11},{4,12},{5,13},{6,14},{7,15},{8,0},{9,1},... | collective-permute-start | bytes 786440 | tf_op jit(solution)/shard_map/ppermute | solution.py:578
  202.3 73.3 %collective-permute-start.31 = (f32[3,4,8,512]{3,2,1,0:T(8,128)S(1)}, f32[3,4,8,512]{3,2,1,0:T(8,128)S(1)}, u32[]{:S(2)}, u32[]{:S(2)}) collective-permute-start(f32[3,4,8,512]{3,2,1,0:T(8,128)S(1)} %get-tuple-element.271), channel_id=1, source_target_pairs={{0,16},{1,17},{2,18},{3,19},{4,20},{5,21},{6,22},{7,23},{8,24},{9,... | collective-permute-start | bytes 589832 | tf_op jit(solution)/shard_map/ppermute | solution.py:578
  203.7 76.9 %collective-permute-start.37 = (f32[3,4,8,512]{3,2,1,0:T(8,128)S(1)}, f32[3,4,8,512]{3,2,1,0:T(8,128)S(1)}, u32[]{:S(2)}, u32[]{:S(2)}) collective-permute-start(f32[3,4,8,512]{3,2,1,0:T(8,128)S(1)} %fusion.9), channel_id=1, source_target_pairs={{0,16},{1,17},{2,18},{3,19},{4,20},{5,21},{6,22},{7,23},{8,24},{9,... | collective-permute-start | bytes 589832 | tf_op jit(solution)/shard_map/ppermute | solution.py:578
  207.2 63.0 %collective-permute-start.36 = (f32[3,4,8,512]{3,2,1,0:T(8,128)S(1)}, f32[3,4,8,512]{3,2,1,0:T(8,128)S(1)}, u32[]{:S(2)}, u32[]{:S(2)}) collective-permute-start(f32[3,4,8,512]{3,2,1,0:T(8,128)S(1)} %fusion.9), channel_id=1, source_target_pairs={{0,8},{1,9},{2,10},{3,11},{4,12},{5,13},{6,14},{7,15},{8,0},{9,1},... | collective-permute-start | bytes 589832 | tf_op jit(solution)/shard_map/ppermute | solution.py:578
  208.7 67.7 %collective-permute-start.32 = (f32[3,4,8,512]{3,2,1,0:T(8,128)S(1)}, f32[3,4,8,512]{3,2,1,0:T(8,128)S(1)}, u32[]{:S(2)}, u32[]{:S(2)}) collective-permute-start(f32[3,4,8,512]{3,2,1,0:T(8,128)S(1)} %collective-permute-done.30), channel_id=1, source_target_pairs={{0,16},{1,17},{2,18},{3,19},{4,20},{5,21},{6,22},{7,23},{8,24},{9,... | collective-permute-start | bytes 589832 | tf_op jit(solution)/shard_map/ppermute | solution.py:578
  210.6 46.6 %collective-permute-start.62 = (f32[2,1,2,8,512]{4,3,2,1,0:T(8,128)S(1)}, f32[2,1,2,8,512]{4,3,2,1,0:T(8,128)S(1)}, u32[]{:S(2)}, u32[]{:S(2)}) collective-permute-start(f32[2,1,2,8,512]{4,3,2,1,0:T(8,128)S(1)} %slice.804), channel_id=1, source_target_pairs={{1,0},{5,1},{9,8},{13,9},{17,16},{21,17},{25,24},{29,25}} | collective-permute-start | bytes 196616 | tf_op jit(solution)/shard_map/ppermute | solution.py:699
  268.9 51.1 %collective-permute-start.60 = (f32[2,4,4,8,512]{4,3,2,1,0:T(8,128)S(1)}, f32[2,4,4,8,512]{4,3,2,1,0:T(8,128)S(1)}, u32[]{:S(2)}, u32[]{:S(2)}) collective-permute-start(f32[2,4,4,8,512]{4,3,2,1,0:T(8,128)S(1)} %maximum_add_fusion), channel_id=1, source_target_pairs={{1,0},{3,1},{5,2},{7,3},{9,8},{11,9},{13,10},{15,11},{17,16},{19,1... | collective-permute-start | bytes 1572872 | tf_op jit(solution)/shard_map/ppermute | solution.py:618
  275.6 45.0 %collective-permute-start.59 = (f32[2,4,4,8,512]{4,3,2,1,0:T(8,128)S(1)}, f32[2,4,4,8,512]{4,3,2,1,0:T(8,128)S(1)}, u32[]{:S(2)}, u32[]{:S(2)}) collective-permute-start(f32[2,4,4,8,512]{4,3,2,1,0:T(8,128)S(1)} %maximum_add_fusion), channel_id=1, source_target_pairs={{0,0},{2,1},{4,2},{6,3},{8,8},{10,9},{12,10},{14,11},{16,16},{18,1... | collective-permute-start | bytes 1572872 | tf_op jit(solution)/shard_map/ppermute | solution.py:617
  280.6 31.1 %collective-permute-start.23 = (f32[4,4,8,512]{3,2,1,0:T(8,128)S(1)}, f32[4,4,8,512]{3,2,1,0:T(8,128)S(1)}, u32[]{:S(2)}, u32[]{:S(2)}) collective-permute-start(f32[4,4,8,512]{3,2,1,0:T(8,128)S(1)} %get-tuple-element.293), channel_id=1, source_target_pairs={{0,16},{1,17},{2,18},{3,19},{4,20},{5,21},{6,22},{7,23},{8,24},{9,... | collective-permute-start | bytes 786440 | tf_op jit(solution)/shard_map/ppermute | solution.py:578
  305.7 26.9 %collective-permute-start.20 = (f32[4,4,8,512]{3,2,1,0:T(8,128)S(1)}, f32[4,4,8,512]{3,2,1,0:T(8,128)S(1)}, u32[]{:S(2)}, u32[]{:S(2)}) collective-permute-start(f32[4,4,8,512]{3,2,1,0:T(8,128)S(1)} %get-tuple-element.292), channel_id=1, source_target_pairs={{0,16},{1,17},{2,18},{3,19},{4,20},{5,21},{6,22},{7,23},{8,24},{9,... | collective-permute-start | bytes 786440 | tf_op jit(solution)/shard_map/ppermute | solution.py:578
  311.7 21.6 %collective-permute-start.21 = (f32[4,4,8,512]{3,2,1,0:T(8,128)S(1)}, f32[4,4,8,512]{3,2,1,0:T(8,128)S(1)}, u32[]{:S(2)}, u32[]{:S(2)}) collective-permute-start(f32[4,4,8,512]{3,2,1,0:T(8,128)S(1)} %collective-permute-done.19), channel_id=1, source_target_pairs={{0,16},{1,17},{2,18},{3,19},{4,20},{5,21},{6,22},{7,23},{8,24},{9,... | collective-permute-start | bytes 786440 | tf_op jit(solution)/shard_map/ppermute | solution.py:578
  320.9 19.8 %collective-permute-start.65 = (f32[5,8,8,512]{3,2,1,0:T(8,128)S(1)}, f32[5,8,8,512]{3,2,1,0:T(8,128)S(1)}, u32[]{:S(2)}, u32[]{:S(2)}) collective-permute-start(f32[5,8,8,512]{3,2,1,0:T(8,128)S(1)} %get-tuple-element.278.refs_8_), channel_id=1, source_target_pairs={{0,8},{1,9},{2,10},{3,11},{8,0},{9,1},{10,2},{11,3},{16,24},{17,25... | collective-permute-start | bytes 1966088 | tf_op jit(solution)/shard_map/ppermute | solution.py:578
  330.2 69.1 %collective-permute-start.72 = (f32[2,2,2,3,4,8,512]{6,5,4,3,2,1,0:T(8,128)S(1)}, f32[2,2,2,3,4,8,512]{6,5,4,3,2,1,0:T(8,128)S(1)}, u32[]{:S(2)}, u32[]{:S(2)}) collective-permute-start(f32[2,2,2,3,4,8,512]{6,5,4,3,2,1,0:T(8,128)S(1)} %pad_maximum_fusion.3.refs_3_.refs_4_), channel_id=1, source_target_pairs={{1,0},{3,1},{5,2},{7,3},{9,8},{11,9},{13,10},{15,11},{17,16},{19,1... | collective-permute-start | bytes 4718600 | tf_op jit(solution)/shard_map/ppermute | solution.py:726
  332.6 66.7 %collective-permute-start.71 = (f32[2,2,2,3,4,8,512]{6,5,4,3,2,1,0:T(8,128)S(1)}, f32[2,2,2,3,4,8,512]{6,5,4,3,2,1,0:T(8,128)S(1)}, u32[]{:S(2)}, u32[]{:S(2)}) collective-permute-start(f32[2,2,2,3,4,8,512]{6,5,4,3,2,1,0:T(8,128)S(1)} %pad_maximum_fusion.3.refs_3_.refs_4_), channel_id=1, source_target_pairs={{0,0},{2,1},{4,2},{6,3},{8,8},{10,9},{12,10},{14,11},{16,16},{18,1... | collective-permute-start | bytes 4718600 | tf_op jit(solution)/shard_map/ppermute | solution.py:725
  333.4 36.2 %collective-permute-start.66 = (f32[5,8,8,512]{3,2,1,0:T(8,128)S(1)}, f32[5,8,8,512]{3,2,1,0:T(8,128)S(1)}, u32[]{:S(2)}, u32[]{:S(2)}) collective-permute-start(f32[5,8,8,512]{3,2,1,0:T(8,128)S(1)} %get-tuple-element.278.refs_8_), channel_id=1, source_target_pairs={{0,16},{1,17},{2,18},{3,19},{8,24},{9,25},{10,26},{11,27},{16,0},{... | collective-permute-start | bytes 1966088 | tf_op jit(solution)/shard_map/ppermute | solution.py:578
  336.5 29.8 %collective-permute-start.69 = (f32[5,8,8,512]{3,2,1,0:T(8,128)S(1)}, f32[5,8,8,512]{3,2,1,0:T(8,128)S(1)}, u32[]{:S(2)}, u32[]{:S(2)}) collective-permute-start(f32[5,8,8,512]{3,2,1,0:T(8,128)S(1)} %get-tuple-element.277.refs_12_), channel_id=1, source_target_pairs={{0,16},{1,17},{2,18},{3,19},{8,24},{9,25},{10,26},{11,27},{16,0},{... | collective-permute-start | bytes 1966088 | tf_op jit(solution)/shard_map/ppermute | solution.py:578
  340.7 39.6 %collective-permute-start.67 = (f32[5,8,8,512]{3,2,1,0:T(8,128)S(1)}, f32[5,8,8,512]{3,2,1,0:T(8,128)S(1)}, u32[]{:S(2)}, u32[]{:S(2)}) collective-permute-start(f32[5,8,8,512]{3,2,1,0:T(8,128)S(1)} %collective-permute-done.65.refs_9_), channel_id=1, source_target_pairs={{0,16},{1,17},{2,18},{3,19},{8,24},{9,25},{10,26},{11,27},{16,0},{... | collective-permute-start | bytes 1966088 | tf_op jit(solution)/shard_map/ppermute | solution.py:578
  366.3 19.0 %collective-permute-start.68 = (f32[5,8,8,512]{3,2,1,0:T(8,128)S(1)}, f32[5,8,8,512]{3,2,1,0:T(8,128)S(1)}, u32[]{:S(2)}, u32[]{:S(2)}) collective-permute-start(f32[5,8,8,512]{3,2,1,0:T(8,128)S(1)} %get-tuple-element.277.refs_12_), channel_id=1, source_target_pairs={{0,8},{1,9},{2,10},{3,11},{8,0},{9,1},{10,2},{11,3},{16,24},{17,25... | collective-permute-start | bytes 1966088 | tf_op jit(solution)/shard_map/ppermute | solution.py:578
  369.6 29.6 %collective-permute-start.70 = (f32[5,8,8,512]{3,2,1,0:T(8,128)S(1)}, f32[5,8,8,512]{3,2,1,0:T(8,128)S(1)}, u32[]{:S(2)}, u32[]{:S(2)}) collective-permute-start(f32[5,8,8,512]{3,2,1,0:T(8,128)S(1)} %collective-permute-done.69.refs_14_), channel_id=1, source_target_pairs={{0,8},{1,9},{2,10},{3,11},{8,0},{9,1},{10,2},{11,3},{16,24},{17,25... | collective-permute-start | bytes 1966088 | tf_op jit(solution)/shard_map/ppermute | solution.py:578
  (81 other events, 870.1 us)

commit v2 on v1

--- a/solution.py
+++ b/solution.py
@@ -128,7 +128,7 @@
 
 def forward_kernel(rows_here, count, scal, fetch, weight, x_ref, *refs):
     tables = dict(zip(CASES, refs[:4]))
-    outs = refs[5:-2]
+    outs = refs[4:-2]
     xb, yb = refs[-2:]
     half_rows = rows_here // 2
     i = pl.program_id(0)
@@ -244,7 +244,7 @@
         d6_self[...] -= 0.5 * e6_rest[...]
 
 
-def forward(grids, scal, weight, after):
+def forward(grids, scal, weight):
     count, rows_here = grids.shape[:2]
     half_rows = rows_here // 2
     tables = forward_tables()
@@ -302,8 +302,7 @@
             num_scalar_prefetch=3,
             grid=(rows_here, count),
             in_specs=[pl.BlockSpec((1, 1, N2, N3 * N4), page)]
-            + [constant(table) for table in ordered]
-            + [pl.BlockSpec(memory_space=pl.ANY)],
+            + [constant(table) for table in ordered],
             out_specs=out_specs,
             scratch_shapes=[
                 pltpu.VMEM((GROUPS, 2 * HB, 2 * (CG + 2) * N4), jnp.bfloat16),
@@ -316,10 +315,10 @@
             flops=10**10, bytes_accessed=60 * 2**20, transcendentals=0
         ),
         name="split_grids",
-    )(scal, fetch, weight, grids, *ordered, after)
-
-
-def coarsest_kernel(count, scal, weight, x_ref, table, out, yb):
+    )(scal, fetch, weight, grids, *ordered)
+
+
+def coarsest_kernel(count, scal, weight, x_ref, table, after, out, yb):
     i = pl.program_id(0)
     mine_x = scal[4 * count]
     mine_y = scal[4 * count + 1]
@@ -348,7 +347,7 @@
                 ]
 
 
-def coarsest(grids, scal, weight):
+def coarsest(grids, scal, weight, after):
     count, rows_here = grids.shape[:2]
     table = forward_tables()[0, 0]
 
@@ -365,6 +364,7 @@
             in_specs=[
                 pl.BlockSpec((1, 1, HB, HC * N4), page),
                 pl.BlockSpec(table.shape, lambda i, *_: (0, 0)),
+                pl.BlockSpec(memory_space=pl.ANY),
             ],
             out_specs=line_spec(lambda i: i),
             scratch_shapes=[pltpu.VMEM((GROUPS, HB, TILE), jnp.float32)],
@@ -375,7 +375,7 @@
             flops=10**8, bytes_accessed=4 * 2**20, transcendentals=0
         ),
         name="split_coarsest",
-    )(scal, weight, grids, table)
+    )(scal, weight, grids, table, after)
 
 
 def rest_spec(blocks, row_of):
@@ -587,7 +587,8 @@
         nearby = exchange(far(1, 0), first, domains)
         onward = far(0, 1) + onward
         nearby = far(0, 0) + nearby
-        reduced.append(nearby + exchange(onward, second, domains))
+        onward = exchange(onward, second, domains)
+        reduced.append(nearby + onward)
     return jnp.stack(reduced)
 
 
@@ -652,17 +653,7 @@
     scal = jnp.concatenate([own_offsets.reshape(-1), place, first[None]])
     sources = dom_size // 2
     quarter_devices = dom_size // 4
-    s4 = coarsest(grids, scal, own_weights)[:, :, :, None]
-    ahead = next_row(s4, quarter_devices)
-    longer = jnp.concatenate([s4, ahead], axis=-3)
-    mids = 0.5 * (longer[..., :-1, :, :] + longer[..., 1:, :, :])
-    spread = jnp.stack([s4, mids], axis=-3).reshape(
-        s4.shape[:-3] + (2 * rows_here,) + s4.shape[-2:]
-    )
-    spread = rows_up(spread, quarter_devices)
-    coarsest_rows = rows_up(spread, sources)
-
-    parts = forward(grids, scal, own_weights, s4)
+    parts = forward(grids, scal, own_weights)
     s5 = dict(zip(SLOTS, parts[:8]))
     s5_low, s5_high, s5_self = parts[8:11]
     e6 = dict(zip(SLOTS, parts[11:19]))
@@ -681,6 +672,29 @@
         slot: d6[slot].at[:, -1:].add(-0.5 * e6_ahead[slot][:SHARED_D]) for slot in SLOTS
     }
 
+    s4 = coarsest(grids, scal, own_weights, s5_self)
+    taken = max(half_rows // 2, 1) + 1
+    lines = 0.0
+    for r in range(4):
+        start = half_rows * r // 2
+        sent = s4[:, :, :, start : start + taken]
+        if sent.shape[3] < taken:
+            sent = jnp.pad(sent, ((0, 0),) * 3 + ((0, taken - sent.shape[3]),) + ((0, 0),) * 2)
+        pairs = [(d, 4 * d + r) for d in range(quarter_devices)]
+        lines = lines + lax.ppermute(sent, "dom", pairs)
+    tops = tuple(r for r in range(4) if half_rows * r // 2 + taken > rows_here)
+    for r in tops:
+        pairs = [((d + 1) % quarter_devices, 4 * d + r) for d in range(quarter_devices)]
+        lines = lines.at[:, :, :, -1:].add(lax.ppermute(s4[:, :, :, :1], "dom", pairs))
+    means = 0.5 * (lines[:, :, :, :-1] + lines[:, :, :, 1:])
+    lines = lines[:, :, :, :-1]
+    if half_rows > 1:
+        coarsest_rows = jnp.stack([lines, means], axis=4).reshape(
+            (2, 2, 2, 1, half_rows) + lines.shape[-2:]
+        )
+    else:
+        between_rows = lax.rem(lax.axis_index("dom"), 2) == 1
+        coarsest_rows = jnp.where(between_rows, means, lines)[:, :, :, None]
     e6 = {slot: e6[slot].at[:1].add(coarsest_rows[slot]) for slot in SLOTS}
 
     if square:

time: 457 us -> 452 us (0.989)
  the two profiles are of different devices: /device:TPU:0 before, /device:TPU:8 now
where the time goes in v2:
time: 452 us; the launch traced here: 450 us
  waiting for transfers between devices  187 us (41%)
  starting transfers between devices  131 us (29%)
  Pallas kernels  105 us (23%)
  other arithmetic  14.9 us (3%)
  local copies, waits for them, and re-layouts  9.72 us (2%)
    ppermute x54, waiting for transfers between devices, exchange(): return lax.ppermute(value, ('half', 'grid', 'dom'), pairs)  105 us
    ppermute x54, starting transfers between devices, exchange(): return lax.ppermute(value, ('half', 'grid', 'dom'), pairs)  81.6 us
    pallas_call x1, Pallas kernels, backward(): pl.pallas_call(lambda *refs: backward_kernel(rows_here, count, *refs), gr...  52.9 us
    pallas_call x1, Pallas kernels, forward(): pl.pallas_call(lambda *refs: forward_kernel(rows_here, count, *refs), gri...  48.1 us
    ppermute x1, waiting for transfers between devices, rows_up(): lax.ppermute(value[..., half_rows:, :, :], 'dom', [(d, 2 * d + 1) for d i...  34.6 us
    ppermute x1, waiting for transfers between devices, per_device(): lax.ppermute(c6_rest, 'dom', [(2 * d + 1, d) for d in range(sources)])  25.6 us
    ppermute x1, starting transfers between devices, rows_down(): low = lax.ppermute(value, 'dom', [(2 * d, d) for d in range(targets)])  19.4 us
    ppermute x1, waiting for transfers between devices, rows_up(): lax.ppermute(value[..., :half_rows, :, :], 'dom', [(d, 2 * d) for d in ra...  12.3 us
  transfers between devices with their start and end apart: 73, of which 28 were waited for; matrix products, arithmetic and copies ran while one was open for 3% of the time, Pallas kernels for 1%

profile of v2, /device:TPU:8, one launch (start us, length us, event | category | flops | bytes accessed | tf_op | source)
XLA Modules:
  0.0 449.8 jit_solution(12448118573858403167)
XLA Ops:
  8.0 48.1 %split_grids.1 = (f32[4,8,8,512]{3,2,1,0:T(8,128)}, f32[4,8,8,512]{3,2,1,0:T(8,128)}, f32[4,8,8,512]{3,2,1,0:T(8,128)}, f32[4,8,8,512]{3,2,1,0:T(8,128)}, f32[4,...) custom-call(s32[20]{0:T(128)} %concatenate.54.refs_0_, ...), custom_call_target="tpu_custom_call" | custom-call | flops 10000000000 | bytes 62914560 | tf_op jit(solution)/shard_map/split_grids/pallas_call | solution.py:299
  58.1 4.4 split_coarsest.1
  71.5 8.1 %collective-permute-done.2 = f32[2,2,2,3,8,512]{5,4,3,2,1,0:T(8,128)S(1)} collective-permute-done((f32[2,2,2,3,8,512]{5,4,3,2,1,0:T(8,128)S(1)}, f32[2,2,2,3,8,512]{5,4,3,2,1,0:T(8,128)S(1)}, u32[]{:S(2)}, u32[]{:S(2)}) %collective-permute-start.2) | collective-permute-done | bytes 393248 | tf_op jit(solution)/shard_map/ppermute | solution.py:684
  79.6 3.7 collective-permute-start.46
  86.5 3.3 collective-permute-start.11
  100.8 3.4 collective-permute-start.16
  108.5 7.7 %collective-permute-done.14 = f32[4,8,8,512]{3,2,1,0:T(8,128)S(1)} collective-permute-done((f32[4,8,8,512]{3,2,1,0:T(8,128)S(1)}, f32[4,8,8,512]{3,2,1,0:T(8,128)S(1)}, u32[]{:S(2)}, u32[]{:S(2)}) %collective-permute-start.14) | collective-permute-done | bytes 524320 | tf_op jit(solution)/shard_map/ppermute | solution.py:578
  118.1 4.4 collective-permute-done.5
  139.2 4.4 collective-permute-done.49
  144.2 34.6 %collective-permute-done.18 = f32[2,4,4,8,512]{4,3,2,1,0:T(8,128)S(1)} collective-permute-done((f32[2,4,4,8,512]{4,3,2,1,0:T(8,128)S(1)}, f32[2,4,4,8,512]{4,3,2,1,0:T(8,128)S(1)}, u32[]{:S(2)}, u32[]{:S(2)}) %collective-permute-start.18) | collective-permute-done | bytes 524320 | tf_op jit(solution)/shard_map/ppermute | solution.py:610
  179.4 12.3 %collective-permute-done.17 = f32[2,4,4,8,512]{4,3,2,1,0:T(8,128)S(1)} collective-permute-done((f32[2,4,4,8,512]{4,3,2,1,0:T(8,128)S(1)}, f32[2,4,4,8,512]{4,3,2,1,0:T(8,128)S(1)}, u32[]{:S(2)}, u32[]{:S(2)}) %collective-permute-start.17) | collective-permute-done | bytes 524320 | tf_op jit(solution)/shard_map/ppermute | solution.py:609
  194.3 8.4 %collective-permute-start.63 = (f32[2,1,2,8,512]{4,3,2,1,0:T(8,128)S(1)}, f32[2,1,2,8,512]{4,3,2,1,0:T(8,128)S(1)}, u32[]{:S(2)}, u32[]{:S(2)}) collective-permute-start(f32[2,1,2,8,512]{4,3,2,1,0:T(8,128)S(1)} %slice.849), channel_id=1, source_target_pairs={{2,0},{6,1},{10,8},{14,9},{18,16},{22,17},{26,24},{30,25}} | collective-permute-start | bytes 196616 | tf_op jit(solution)/shard_map/ppermute | solution.py:713
  209.8 6.4 %collective-permute-done.28 = f32[3,4,8,512]{3,2,1,0:T(8,128)S(1)} collective-permute-done((f32[3,4,8,512]{3,2,1,0:T(8,128)S(1)}, f32[3,4,8,512]{3,2,1,0:T(8,128)S(1)}, u32[]{:S(2)}, u32[]{:S(2)}) %collective-permute-start.28) | collective-permute-done | bytes 196640 | tf_op jit(solution)/shard_map/ppermute | solution.py:578
  221.7 3.4 collective-permute-done.58
  225.1 2.8 collective-permute-start.52
  229.5 5.6 %collective-permute-done.52 = f32[4,4,8,512]{3,2,1,0:T(8,128)S(1)} collective-permute-done((f32[4,4,8,512]{3,2,1,0:T(8,128)S(1)}, f32[4,4,8,512]{3,2,1,0:T(8,128)S(1)}, u32[]{:S(2)}, u32[]{:S(2)}) %collective-permute-start.52) | collective-permute-done | bytes 262176 | tf_op jit(solution)/shard_map/ppermute | solution.py:578
  241.5 19.4 %collective-permute-start.59 = (f32[2,4,4,8,512]{4,3,2,1,0:T(8,128)S(1)}, f32[2,4,4,8,512]{4,3,2,1,0:T(8,128)S(1)}, u32[]{:S(2)}, u32[]{:S(2)}) collective-permute-start(f32[2,4,4,8,512]{4,3,2,1,0:T(8,128)S(1)} %maximum_add_fusion), channel_id=1, source_target_pairs={{0,0},{2,1},{4,2},{6,3},{8,8},{10,9},{12,10},{14,11},{16,16},{18,1... | collective-permute-start | bytes 1572872 | tf_op jit(solution)/shard_map/ppermute | solution.py:618
  263.8 6.4 %collective-permute-done.24 = f32[4,4,8,512]{3,2,1,0:T(8,128)S(1)} collective-permute-done((f32[4,4,8,512]{3,2,1,0:T(8,128)S(1)}, f32[4,4,8,512]{3,2,1,0:T(8,128)S(1)}, u32[]{:S(2)}, u32[]{:S(2)}) %collective-permute-start.24) | collective-permute-done | bytes 262176 | tf_op jit(solution)/shard_map/ppermute | solution.py:578
  274.2 3.6 collective-permute-start.66
  277.9 3.5 collective-permute-done.35
  284.0 3.5 collective-permute-done.36
  290.2 7.6 %collective-permute-done.37 = f32[3,4,8,512]{3,2,1,0:T(8,128)S(1)} collective-permute-done((f32[3,4,8,512]{3,2,1,0:T(8,128)S(1)}, f32[3,4,8,512]{3,2,1,0:T(8,128)S(1)}, u32[]{:S(2)}, u32[]{:S(2)}) %collective-permute-start.37) | collective-permute-done | bytes 196640 | tf_op jit(solution)/shard_map/ppermute | solution.py:578
  302.2 11.1 %collective-permute-done.40 = f32[7,1,8,512]{3,2,0,1:T(8,128)S(1)} collective-permute-done((f32[7,1,8,512]{3,2,0,1:T(8,128)S(1)}, f32[7,1,8,512]{3,2,0,1:T(8,128)S(1)}, u32[]{:S(2)}, u32[]{:S(2)}) %collective-permute-start.40) | collective-permute-done | bytes 114720 | tf_op jit(solution)/shard_map/ppermute | solution.py:578
  314.0 4.1 collective-permute-done.43
  320.6 3.6 collective-permute-start.69
  334.4 5.7 %collective-permute-done.69.refs_14_ = f32[5,8,8,512]{3,2,1,0:T(8,128)S(1)} collective-permute-done((f32[5,8,8,512]{3,2,1,0:T(8,128)S(1)}, f32[5,8,8,512]{3,2,1,0:T(8,128)S(1)}, u32[]{:S(2)}, u32[]{:S(2)}) %collective-permute-start.69) | collective-permute-done | bytes 655392 | tf_op jit(solution)/shard_map/ppermute | solution.py:578
  342.7 3.2 collective-permute-start.70
  346.0 6.5 %collective-permute-done.67.refs_11_ = f32[5,8,8,512]{3,2,1,0:T(8,128)S(1)} collective-permute-done((f32[5,8,8,512]{3,2,1,0:T(8,128)S(1)}, f32[5,8,8,512]{3,2,1,0:T(8,128)S(1)}, u32[]{:S(2)}, u32[]{:S(2)}) %collective-permute-start.67) | collective-permute-done | bytes 655392 | tf_op jit(solution)/shard_map/ppermute | solution.py:578
  352.5 7.1 %collective-permute-done.68.refs_13_ = f32[5,8,8,512]{3,2,1,0:T(8,128)S(1)} collective-permute-done((f32[5,8,8,512]{3,2,1,0:T(8,128)S(1)}, f32[5,8,8,512]{3,2,1,0:T(8,128)S(1)}, u32[]{:S(2)}, u32[]{:S(2)}) %collective-permute-start.68) | collective-permute-done | bytes 655392 | tf_op jit(solution)/shard_map/ppermute | solution.py:578
  359.6 9.8 %collective-permute-done.70.refs_15_ = f32[5,8,8,512]{3,2,1,0:T(8,128)S(1)} collective-permute-done((f32[5,8,8,512]{3,2,1,0:T(8,128)S(1)}, f32[5,8,8,512]{3,2,1,0:T(8,128)S(1)}, u32[]{:S(2)}, u32[]{:S(2)}) %collective-permute-start.70) | collective-permute-done | bytes 655392 | tf_op jit(solution)/shard_map/ppermute | solution.py:578
  369.4 25.6 %collective-permute-done.72.refs_17_ = f32[2,2,2,3,4,8,512]{6,5,4,3,2,1,0:T(8,128)S(1)} collective-permute-done((f32[2,2,2,3,4,8,512]{6,5,4,3,2,1,0:T(8,128)S(1)}, f32[2,2,2,3,4,8,512]{6,5,4,3,2,1,0:T(8,128)S(1)}, u32[]{:S(2)}, u32[]{:S(2)}) %collective-permute-start.72) | collective-permute-done | bytes 1572896 | tf_op jit(solution)/shard_map/ppermute | solution.py:740
  396.7 52.9 %join_grids.1 = f32[4,8,64,4096]{3,2,1,0:T(8,128)} custom-call(s32[20]{0:T(128)} %concatenate.54.refs_0_, f32[2,2,2,4,4,8,512]{6,5,4,3,2,1,0:T(8,128)} %pad_maximum_fusion.refs_1_.refs_2_, f32[2,2,2,4,4,8,512]{6,5,4,3,2,1,0:T(8,128)} %pad_maximum_fusion.refs_1_.refs_2_, f32[2,2,2,3,4,8,512]{6,5,4,3,2,1,0:T(8,128)} %copy-done, ...), custom_call_target="tpu_custom_call" | custom-call | flops 10000000000 | bytes 62914560 | tf_op jit(solution)/shard_map/join_grids/pallas_call | solution.py:536
  (314 shorter events, 113.6 us)
Async XLA Ops:
  56.1 30.2 %collective-permute-start.12 = (f32[4,8,8,512]{3,2,1,0:T(8,128)}, f32[4,8,8,512]{3,2,1,0:T(8,128)S(1)}, u32[]{:S(2)}, u32[]{:S(2)}) collective-permute-start(f32[4,8,8,512]{3,2,1,0:T(8,128)} %get-tuple-element.264), channel_id=1, source_target_pairs={{0,16},{1,17},{2,18},{3,19},{8,24},{9,25},{10,26},{11,27},{16,0},{... | collective-permute-start | bytes 1572872 | tf_op jit(solution)/shard_map/ppermute | solution.py:578
  69.6 20.3 %collective-permute-start.15 = (f32[4,8,8,512]{3,2,1,0:T(8,128)S(1)}, f32[4,8,8,512]{3,2,1,0:T(8,128)S(1)}, u32[]{:S(2)}, u32[]{:S(2)}) collective-permute-start(f32[4,8,8,512]{3,2,1,0:T(8,128)S(1)} %copy-done.38), channel_id=1, source_target_pairs={{0,8},{1,9},{2,10},{3,11},{8,0},{9,1},{10,2},{11,3},{16,24},{17,25... | collective-permute-start | bytes 1572872 | tf_op jit(solution)/shard_map/ppermute | solution.py:578
  86.5 17.8 %collective-permute-start.11 = (f32[4,8,8,512]{3,2,1,0:T(8,128)S(1)}, f32[4,8,8,512]{3,2,1,0:T(8,128)S(1)}, u32[]{:S(2)}, u32[]{:S(2)}) collective-permute-start(f32[4,8,8,512]{3,2,1,0:T(8,128)S(1)} %copy-done.37), channel_id=1, source_target_pairs={{0,16},{1,17},{2,18},{3,19},{8,24},{9,25},{10,26},{11,27},{16,0},{... | collective-permute-start | bytes 1572872 | tf_op jit(solution)/shard_map/ppermute | solution.py:578
  98.2 18.0 %collective-permute-start.14 = (f32[4,8,8,512]{3,2,1,0:T(8,128)S(1)}, f32[4,8,8,512]{3,2,1,0:T(8,128)S(1)}, u32[]{:S(2)}, u32[]{:S(2)}) collective-permute-start(f32[4,8,8,512]{3,2,1,0:T(8,128)S(1)} %copy-done.36), channel_id=1, source_target_pairs={{0,8},{1,9},{2,10},{3,11},{8,0},{9,1},{10,2},{11,3},{16,24},{17,25... | collective-permute-start | bytes 1572872 | tf_op jit(solution)/shard_map/ppermute | solution.py:578
  100.8 25.2 %collective-permute-start.16 = (f32[4,8,8,512]{3,2,1,0:T(8,128)S(1)}, f32[4,8,8,512]{3,2,1,0:T(8,128)S(1)}, u32[]{:S(2)}, u32[]{:S(2)}) collective-permute-start(f32[4,8,8,512]{3,2,1,0:T(8,128)S(1)} %add.288), channel_id=1, source_target_pairs={{0,16},{1,17},{2,18},{3,19},{8,24},{9,25},{10,26},{11,27},{16,0},{... | collective-permute-start | bytes 1572872 | tf_op jit(solution)/shard_map/ppermute | solution.py:578
  104.3 18.2 %collective-permute-start.5 = (f32[4,4,8,512]{3,2,1,0:T(8,128)S(1)}, f32[4,4,8,512]{3,2,1,0:T(8,128)S(1)}, u32[]{:S(2)}, u32[]{:S(2)}) collective-permute-start(f32[4,4,8,512]{3,2,1,0:T(8,128)S(1)} %get-tuple-element.306), channel_id=1, source_target_pairs={{0,16},{1,17},{2,18},{3,19},{4,20},{5,21},{6,22},{7,23},{8,24},{9,... | collective-permute-start | bytes 786440 | tf_op jit(solution)/shard_map/ppermute | solution.py:578
  104.9 19.0 %collective-permute-start.7 = (f32[4,4,8,512]{3,2,1,0:T(8,128)S(1)}, f32[4,4,8,512]{3,2,1,0:T(8,128)S(1)}, u32[]{:S(2)}, u32[]{:S(2)}) collective-permute-start(f32[4,4,8,512]{3,2,1,0:T(8,128)S(1)} %add.275), channel_id=1, source_target_pairs={{0,8},{1,9},{2,10},{3,11},{4,12},{5,13},{6,14},{7,15},{8,0},{9,1},... | collective-permute-start | bytes 786440 | tf_op jit(solution)/shard_map/ppermute | solution.py:578
  106.5 21.6 %collective-permute-start.48 = (f32[4,4,8,512]{3,2,1,0:T(8,128)S(1)}, f32[4,4,8,512]{3,2,1,0:T(8,128)S(1)}, u32[]{:S(2)}, u32[]{:S(2)}) collective-permute-start(f32[4,4,8,512]{3,2,1,0:T(8,128)S(1)} %get-tuple-element.299), channel_id=1, source_target_pairs={{0,16},{1,17},{2,18},{3,19},{4,20},{5,21},{6,22},{7,23},{8,24},{9,... | collective-permute-start | bytes 786440 | tf_op jit(solution)/shard_map/ppermute | solution.py:578
  116.2 75.7 %collective-permute-start.25 = (f32[2,2,2,3,4,8,512]{6,5,4,3,2,1,0:T(8,128)S(1)}, f32[2,2,2,3,4,8,512]{6,5,4,3,2,1,0:T(8,128)S(1)}, u32[]{:S(2)}, u32[]{:S(2)}) collective-permute-start(f32[2,2,2,3,4,8,512]{6,5,4,3,2,1,0:T(8,128)S(1)} %copy-done.35), channel_id=1, source_target_pairs={{0,0},{1,2},{2,4},{3,6},{8,8},{9,10},{10,12},{11,14},{16,16},{17,1... | collective-permute-start | bytes 4718600 | tf_op jit(solution)/shard_map/ppermute | solution.py:663
  122.5 69.5 %collective-permute-start.26 = (f32[2,2,2,3,4,8,512]{6,5,4,3,2,1,0:T(8,128)S(1)}, f32[2,2,2,3,4,8,512]{6,5,4,3,2,1,0:T(8,128)S(1)}, u32[]{:S(2)}, u32[]{:S(2)}) collective-permute-start(f32[2,2,2,3,4,8,512]{6,5,4,3,2,1,0:T(8,128)S(1)} %copy-done.34), channel_id=1, source_target_pairs={{0,1},{1,3},{2,5},{3,7},{8,9},{9,11},{10,13},{11,15},{16,17},{17,1... | collective-permute-start | bytes 4718600 | tf_op jit(solution)/shard_map/ppermute | solution.py:664
  131.5 47.2 %collective-permute-start.18 = (f32[2,4,4,8,512]{4,3,2,1,0:T(8,128)S(1)}, f32[2,4,4,8,512]{4,3,2,1,0:T(8,128)S(1)}, u32[]{:S(2)}, u32[]{:S(2)}) collective-permute-start(f32[2,4,4,8,512]{4,3,2,1,0:T(8,128)S(1)} %get-tuple-element.289), channel_id=1, source_target_pairs={{0,1},{1,3},{2,5},{3,7},{8,9},{9,11},{10,13},{11,15},{16,17},{17,1... | collective-permute-start | bytes 1572872 | tf_op jit(solution)/shard_map/ppermute | solution.py:610
  135.2 56.5 %collective-permute-start.17 = (f32[2,4,4,8,512]{4,3,2,1,0:T(8,128)S(1)}, f32[2,4,4,8,512]{4,3,2,1,0:T(8,128)S(1)}, u32[]{:S(2)}, u32[]{:S(2)}) collective-permute-start(f32[2,4,4,8,512]{4,3,2,1,0:T(8,128)S(1)} %get-tuple-element.290), channel_id=1, source_target_pairs={{0,0},{1,2},{2,4},{3,6},{8,8},{9,10},{10,12},{11,14},{16,16},{17,1... | collective-permute-start | bytes 1572872 | tf_op jit(solution)/shard_map/ppermute | solution.py:609
  143.6 65.8 %collective-permute-start.57 = (f32[4,4,8,512]{3,2,1,0:T(8,128)S(1)}, f32[4,4,8,512]{3,2,1,0:T(8,128)S(1)}, u32[]{:S(2)}, u32[]{:S(2)}) collective-permute-start(f32[4,4,8,512]{3,2,1,0:T(8,128)S(1)} %add_add_fusion.2), channel_id=1, source_target_pairs={{0,16},{1,17},{2,18},{3,19},{4,20},{5,21},{6,22},{7,23},{8,24},{9,... | collective-permute-start | bytes 786440 | tf_op jit(solution)/shard_map/ppermute | solution.py:578
  178.7 28.7 %collective-permute-start.56 = (f32[4,4,8,512]{3,2,1,0:T(8,128)S(1)}, f32[4,4,8,512]{3,2,1,0:T(8,128)S(1)}, u32[]{:S(2)}, u32[]{:S(2)}) collective-permute-start(f32[4,4,8,512]{3,2,1,0:T(8,128)S(1)} %add_add_fusion.2), channel_id=1, source_target_pairs={{0,8},{1,9},{2,10},{3,11},{4,12},{5,13},{6,14},{7,15},{8,0},{9,1},... | collective-permute-start | bytes 786440 | tf_op jit(solution)/shard_map/ppermute | solution.py:578
  191.7 36.4 %collective-permute-start.51 = (f32[4,4,8,512]{3,2,1,0:T(8,128)S(1)}, f32[4,4,8,512]{3,2,1,0:T(8,128)S(1)}, u32[]{:S(2)}, u32[]{:S(2)}) collective-permute-start(f32[4,4,8,512]{3,2,1,0:T(8,128)S(1)} %add_add_fusion.3), channel_id=1, source_target_pairs={{0,16},{1,17},{2,18},{3,19},{4,20},{5,21},{6,22},{7,23},{8,24},{9,... | collective-permute-start | bytes 786440 | tf_op jit(solution)/shard_map/ppermute | solution.py:578
  205.3 57.4 %collective-permute-start.20 = (f32[4,4,8,512]{3,2,1,0:T(8,128)S(1)}, f32[4,4,8,512]{3,2,1,0:T(8,128)S(1)}, u32[]{:S(2)}, u32[]{:S(2)}) collective-permute-start(f32[4,4,8,512]{3,2,1,0:T(8,128)S(1)} %get-tuple-element.303), channel_id=1, source_target_pairs={{0,16},{1,17},{2,18},{3,19},{4,20},{5,21},{6,22},{7,23},{8,24},{9,... | collective-permute-start | bytes 786440 | tf_op jit(solution)/shard_map/ppermute | solution.py:578
  218.4 23.1 %collective-permute-start.23 = (f32[4,4,8,512]{3,2,1,0:T(8,128)S(1)}, f32[4,4,8,512]{3,2,1,0:T(8,128)S(1)}, u32[]{:S(2)}, u32[]{:S(2)}) collective-permute-start(f32[4,4,8,512]{3,2,1,0:T(8,128)S(1)} %get-tuple-element.304), channel_id=1, source_target_pairs={{0,16},{1,17},{2,18},{3,19},{4,20},{5,21},{6,22},{7,23},{8,24},{9,... | collective-permute-start | bytes 786440 | tf_op jit(solution)/shard_map/ppermute | solution.py:578
  235.1 25.9 %collective-permute-start.29 = (f32[3,4,8,512]{3,2,1,0:T(8,128)S(1)}, f32[3,4,8,512]{3,2,1,0:T(8,128)S(1)}, u32[]{:S(2)}, u32[]{:S(2)}) collective-permute-start(f32[3,4,8,512]{3,2,1,0:T(8,128)S(1)} %fusion.9), channel_id=1, source_target_pairs={{0,8},{1,9},{2,10},{3,11},{4,12},{5,13},{6,14},{7,15},{8,0},{9,1},... | collective-permute-start | bytes 589832 | tf_op jit(solution)/shard_map/ppermute | solution.py:578
  236.9 26.3 %collective-permute-start.21 = (f32[4,4,8,512]{3,2,1,0:T(8,128)S(1)}, f32[4,4,8,512]{3,2,1,0:T(8,128)S(1)}, u32[]{:S(2)}, u32[]{:S(2)}) collective-permute-start(f32[4,4,8,512]{3,2,1,0:T(8,128)S(1)} %collective-permute-done.19), channel_id=1, source_target_pairs={{0,16},{1,17},{2,18},{3,19},{4,20},{5,21},{6,22},{7,23},{8,24},{9,... | collective-permute-start | bytes 786440 | tf_op jit(solution)/shard_map/ppermute | solution.py:578
  240.2 33.4 %collective-permute-start.60 = (f32[2,4,4,8,512]{4,3,2,1,0:T(8,128)S(1)}, f32[2,4,4,8,512]{4,3,2,1,0:T(8,128)S(1)}, u32[]{:S(2)}, u32[]{:S(2)}) collective-permute-start(f32[2,4,4,8,512]{4,3,2,1,0:T(8,128)S(1)} %maximum_add_fusion), channel_id=1, source_target_pairs={{1,0},{3,1},{5,2},{7,3},{9,8},{11,9},{13,10},{15,11},{17,16},{19,1... | collective-permute-start | bytes 1572872 | tf_op jit(solution)/shard_map/ppermute | solution.py:619
  241.5 32.4 %collective-permute-start.59 = (f32[2,4,4,8,512]{4,3,2,1,0:T(8,128)S(1)}, f32[2,4,4,8,512]{4,3,2,1,0:T(8,128)S(1)}, u32[]{:S(2)}, u32[]{:S(2)}) collective-permute-start(f32[2,4,4,8,512]{4,3,2,1,0:T(8,128)S(1)} %maximum_add_fusion), channel_id=1, source_target_pairs={{0,0},{2,1},{4,2},{6,3},{8,8},{10,9},{12,10},{14,11},{16,16},{18,1... | collective-permute-start | bytes 1572872 | tf_op jit(solution)/shard_map/ppermute | solution.py:618
  263.2 24.3 %collective-permute-start.31 = (f32[3,4,8,512]{3,2,1,0:T(8,128)S(1)}, f32[3,4,8,512]{3,2,1,0:T(8,128)S(1)}, u32[]{:S(2)}, u32[]{:S(2)}) collective-permute-start(f32[3,4,8,512]{3,2,1,0:T(8,128)S(1)} %get-tuple-element.281), channel_id=1, source_target_pairs={{0,16},{1,17},{2,18},{3,19},{4,20},{5,21},{6,22},{7,23},{8,24},{9,... | collective-permute-start | bytes 589832 | tf_op jit(solution)/shard_map/ppermute | solution.py:578
  274.2 68.5 %collective-permute-start.66 = (f32[5,8,8,512]{3,2,1,0:T(8,128)S(1)}, f32[5,8,8,512]{3,2,1,0:T(8,128)S(1)}, u32[]{:S(2)}, u32[]{:S(2)}) collective-permute-start(f32[5,8,8,512]{3,2,1,0:T(8,128)S(1)} %get-tuple-element.288.refs_8_), channel_id=1, source_target_pairs={{0,16},{1,17},{2,18},{3,19},{8,24},{9,25},{10,26},{11,27},{16,0},{... | collective-permute-start | bytes 1966088 | tf_op jit(solution)/shard_map/ppermute | solution.py:578
  287.5 43.6 %collective-permute-start.65 = (f32[5,8,8,512]{3,2,1,0:T(8,128)S(1)}, f32[5,8,8,512]{3,2,1,0:T(8,128)S(1)}, u32[]{:S(2)}, u32[]{:S(2)}) collective-permute-start(f32[5,8,8,512]{3,2,1,0:T(8,128)S(1)} %get-tuple-element.288.refs_8_), channel_id=1, source_target_pairs={{0,8},{1,9},{2,10},{3,11},{8,0},{9,1},{10,2},{11,3},{16,24},{17,25... | collective-permute-start | bytes 1966088 | tf_op jit(solution)/shard_map/ppermute | solution.py:578
  297.8 22.0 %collective-permute-start.38 = (f32[3,4,8,512]{3,2,1,0:T(8,128)S(1)}, f32[3,4,8,512]{3,2,1,0:T(8,128)S(1)}, u32[]{:S(2)}, u32[]{:S(2)}) collective-permute-start(f32[3,4,8,512]{3,2,1,0:T(8,128)S(1)} %collective-permute-done.37), channel_id=1, source_target_pairs={{0,8},{1,9},{2,10},{3,11},{4,12},{5,13},{6,14},{7,15},{8,0},{9,1},... | collective-permute-start | bytes 589832 | tf_op jit(solution)/shard_map/ppermute | solution.py:578
  299.9 20.7 %collective-permute-start.41 = (f32[7,1,8,512]{3,2,0,1:T(8,128)S(1)}, f32[7,1,8,512]{3,2,0,1:T(8,128)S(1)}, u32[]{:S(2)}, u32[]{:S(2)}) collective-permute-start(f32[7,1,8,512]{3,2,0,1:T(8,128)S(1)} %get-tuple-element.317), channel_id=1, source_target_pairs={{0,16},{1,17},{2,18},{3,19},{4,20},{5,21},{6,22},{7,23},{8,24},{9,... | collective-permute-start | bytes 344072 | tf_op jit(solution)/shard_map/ppermute | solution.py:578
  320.6 19.5 %collective-permute-start.69 = (f32[5,8,8,512]{3,2,1,0:T(8,128)S(1)}, f32[5,8,8,512]{3,2,1,0:T(8,128)S(1)}, u32[]{:S(2)}, u32[]{:S(2)}) collective-permute-start(f32[5,8,8,512]{3,2,1,0:T(8,128)S(1)} %get-tuple-element.287.refs_12_), channel_id=1, source_target_pairs={{0,16},{1,17},{2,18},{3,19},{8,24},{9,25},{10,26},{11,27},{16,0},{... | collective-permute-start | bytes 1966088 | tf_op jit(solution)/shard_map/ppermute | solution.py:578
  325.9 69.1 %collective-permute-start.72 = (f32[2,2,2,3,4,8,512]{6,5,4,3,2,1,0:T(8,128)S(1)}, f32[2,2,2,3,4,8,512]{6,5,4,3,2,1,0:T(8,128)S(1)}, u32[]{:S(2)}, u32[]{:S(2)}) collective-permute-start(f32[2,2,2,3,4,8,512]{6,5,4,3,2,1,0:T(8,128)S(1)} %pad_maximum_fusion.2.refs_3_.refs_4_), channel_id=1, source_target_pairs={{1,0},{3,1},{5,2},{7,3},{9,8},{11,9},{13,10},{15,11},{17,16},{19,1... | collective-permute-start | bytes 4718600 | tf_op jit(solution)/shard_map/ppermute | solution.py:740
  329.1 66.0 %collective-permute-start.71 = (f32[2,2,2,3,4,8,512]{6,5,4,3,2,1,0:T(8,128)S(1)}, f32[2,2,2,3,4,8,512]{6,5,4,3,2,1,0:T(8,128)S(1)}, u32[]{:S(2)}, u32[]{:S(2)}) collective-permute-start(f32[2,2,2,3,4,8,512]{6,5,4,3,2,1,0:T(8,128)S(1)} %pad_maximum_fusion.2.refs_3_.refs_4_), channel_id=1, source_target_pairs={{0,0},{2,1},{4,2},{6,3},{8,8},{10,9},{12,10},{14,11},{16,16},{18,1... | collective-permute-start | bytes 4718600 | tf_op jit(solution)/shard_map/ppermute | solution.py:739
  331.1 21.3 %collective-permute-start.67 = (f32[5,8,8,512]{3,2,1,0:T(8,128)S(1)}, f32[5,8,8,512]{3,2,1,0:T(8,128)S(1)}, u32[]{:S(2)}, u32[]{:S(2)}) collective-permute-start(f32[5,8,8,512]{3,2,1,0:T(8,128)S(1)} %collective-permute-done.65.refs_9_), channel_id=1, source_target_pairs={{0,16},{1,17},{2,18},{3,19},{8,24},{9,25},{10,26},{11,27},{16,0},{... | collective-permute-start | bytes 1966088 | tf_op jit(solution)/shard_map/ppermute | solution.py:578
  340.1 19.5 %collective-permute-start.68 = (f32[5,8,8,512]{3,2,1,0:T(8,128)S(1)}, f32[5,8,8,512]{3,2,1,0:T(8,128)S(1)}, u32[]{:S(2)}, u32[]{:S(2)}) collective-permute-start(f32[5,8,8,512]{3,2,1,0:T(8,128)S(1)} %get-tuple-element.287.refs_12_), channel_id=1, source_target_pairs={{0,8},{1,9},{2,10},{3,11},{8,0},{9,1},{10,2},{11,3},{16,24},{17,25... | collective-permute-start | bytes 1966088 | tf_op jit(solution)/shard_map/ppermute | solution.py:578
  342.7 26.7 %collective-permute-start.70 = (f32[5,8,8,512]{3,2,1,0:T(8,128)S(1)}, f32[5,8,8,512]{3,2,1,0:T(8,128)S(1)}, u32[]{:S(2)}, u32[]{:S(2)}) collective-permute-start(f32[5,8,8,512]{3,2,1,0:T(8,128)S(1)} %collective-permute-done.69.refs_14_), channel_id=1, source_target_pairs={{0,8},{1,9},{2,10},{3,11},{8,0},{9,1},{10,2},{11,3},{16,24},{17,25... | collective-permute-start | bytes 1966088 | tf_op jit(solution)/shard_map/ppermute | solution.py:578
  (81 other events, 898.7 us)
